TPU v7x, 512 devices: a whole 4x4x16 slice. The times are simulated.
512 devices in a mesh: adv: 64 (over z, y_lo, core), imp: 8 (over x, y_hi).
Axes of the slice: x: 4, y: 4 (y_hi: 2, y_lo: 2; y = y_hi * 2 + y_lo), z: 16, core: 2. Of those that a mesh axis runs over, the one named last changes fastest.
Arguments:
- values: bfloat16 [16384, 16384], P('adv', 'imp'), may hold values from 0 to 4
- limits: float32 [16384], P('adv'), may hold values from 0.05 to 3
- start_pace: float32 [16384], P('adv'), may hold values from 0.3 to 1
- reserve: float32 [16384], P('imp'), may hold values from 0.2 to 1.2
Outputs:
- pace: float32 [16384], P('adv')
- prices: float32 [16384], P('imp')
All inputs are finite; a program needn't handle non-finite values.
Results may differ from a plain program's by a relative error of at most 0.0003.
Values sent between devices are 32-bit elements; how exact they have to be, the bound alone decides.
No kernel may reach another device: no remote copies, remote signals or barrier semaphores. Data moves between devices by JAX's collectives and lax.ppermute only.
A program may use at most 64 MiB of HBM per device.

v0:
```python
import jax
import jax.numpy as jnp
from jax import lax
from jax.sharding import PartitionSpec as P

ROUNDS = 2


EPS = 0.015


def log_totals(score, rlog):
    top = jnp.maximum(lax.pmax(jnp.max(score, axis=0), "adv"), rlog)
    total = lax.psum(jnp.sum(jnp.exp(score - top[None, :]), axis=0), "adv")
    return top + jnp.log(total + jnp.exp(rlog - top))


def update_pace(partial_value, pace, limits):
    spend = lax.psum(partial_value, "imp")
    return jnp.minimum(1.0, pace * jnp.sqrt(limits / spend))


def on_device(values, limits, start_pace, reserve):
    pace = start_pace
    rlog = reserve / EPS
    prices = jnp.zeros_like(reserve)
    for step in range(ROUNDS):
        bid = pace[:, None] * values.astype(jnp.float32)
        score = bid / EPS
        lse = log_totals(score, rlog)
        prices = EPS * lse
        partial_value = jnp.sum(jnp.exp(score - lse[None, :]) * bid, axis=1)
        pace = update_pace(partial_value, pace, limits)
    return (pace, prices)


def solution(mesh):
    placed = (P("adv", "imp"), P("adv"), P("adv"), P("imp"))
    return jax.shard_map(
        on_device, mesh=mesh, in_specs=placed, out_specs=(P("adv"), P("imp")), check_vma=False
    )
```

profile of v0, /device:TPU:1, one launch (start us, length us, event | category | flops | bytes accessed | tf_op | source)
XLA Modules:
  0.0 483.7 jit_solution(3933915852392076047)
XLA Ops:
  0.6 0.0 copy-start
  0.6 0.0 copy-start.1
  0.6 0.0 copy-start.2
  0.7 1.7 fusion.4
  2.3 114.3 %pmax.14 = f32[2048]{0:T(1024)S(1)} all-reduce(f32[2048]{0:T(1024)S(1)} %fusion.4), channel_id=1, replica_groups=mesh['adv'=64,'imp'=8] {'adv'}, use_global_device_ids=true, to_apply=%region_1.0 | all-reduce | flops 2048 | bytes 16384 | tf_op jit(solution)/shard_map/pmax | solution.py:13
  116.6 0.0 copy-done.1
  116.7 0.0 copy-done
  116.7 0.0 copy-done.2
  116.7 0.0 copy-start.3
  116.7 0.6 fusion.15
  117.3 109.9 %psum.28 = f32[2048]{0:T(1024)S(1)} all-reduce(f32[2048]{0:T(1024)S(1)} %fusion.15), channel_id=1, replica_groups=mesh['adv'=64,'imp'=8] {'adv'}, use_global_device_ids=true, to_apply=%region_3.0 | all-reduce | flops 2048 | bytes 16384 | tf_op jit(solution)/shard_map/psum | solution.py:14
  227.2 0.7 fusion.17
  227.9 20.3 %psum.29 = f32[256]{0:T(256)S(1)} all-reduce(f32[256]{0:T(256)S(1)} %fusion.17), channel_id=1, replica_groups=mesh['adv'=64,'imp'=8] {'imp'}, use_global_device_ids=true, to_apply=%region_5.0 | all-reduce | flops 256 | bytes 2048 | tf_op jit(solution)/shard_map/psum | solution.py:19
  248.2 0.0 copy-done.3
  248.2 0.4 fusion.9
  248.6 110.5 %pmax.15 = f32[2048]{0:T(1024)S(1)} all-reduce(f32[2048]{0:T(1024)S(1)} %fusion.9), channel_id=1, replica_groups=mesh['adv'=64,'imp'=8] {'adv'}, use_global_device_ids=true, to_apply=%region_7.0 | all-reduce | flops 2048 | bytes 16384 | tf_op jit(solution)/shard_map/pmax | solution.py:13
  359.1 0.6 fusion.11
  359.6 106.7 %psum.30 = f32[2048]{0:T(1024)S(1)} all-reduce(f32[2048]{0:T(1024)S(1)} %fusion.11), channel_id=1, replica_groups=mesh['adv'=64,'imp'=8] {'adv'}, use_global_device_ids=true, to_apply=%region_9.0 | all-reduce | flops 2048 | bytes 16384 | tf_op jit(solution)/shard_map/psum | solution.py:14
  466.4 0.6 broadcast_multiply_fusion
  467.0 0.7 fusion.13
  467.7 15.5 %psum.31 = f32[256]{0:T(256)S(1)} all-reduce(f32[256]{0:T(256)S(1)} %fusion.13), channel_id=1, replica_groups=mesh['adv'=64,'imp'=8] {'imp'}, use_global_device_ids=true, to_apply=%region_11.0 | all-reduce | flops 256 | bytes 2048 | tf_op jit(solution)/shard_map/psum | solution.py:19
  483.2 0.6 multiply_minimum_fusion
  (4 shorter events, 0.0 us)
Async XLA Ops:
  0.6 116.0 %copy-start = (bf16[256,2048]{1,0:T(8,128)(2,1)S(1)}, bf16[256,2048]{1,0:T(8,128)(2,1)}, u32[]{:S(2)}) copy-start(bf16[256,2048]{1,0:T(8,128)(2,1)} %param.4) | copy-start | bytes 3145732
  0.6 116.0 %copy-start.1 = (f32[2048]{0:T(1024)S(1)}, f32[2048]{0:T(1024)}, u32[]{:S(2)}) copy-start(f32[2048]{0:T(1024)} %param.7) | copy-start | bytes 24580
  0.6 116.0 %copy-start.2 = (f32[256]{0:T(256)S(1)}, f32[256]{0:T(256)}, u32[]{:S(2)}) copy-start(f32[256]{0:T(256)} %param.6) | copy-start | bytes 3076
  116.7 131.5 %copy-start.3 = (f32[256]{0:T(256)S(1)}, f32[256]{0:T(256)}, u32[]{:S(2)}) copy-start(f32[256]{0:T(256)} %param.5) | copy-start | bytes 3076
where the time goes:
time: 487 us; the launch traced here: 484 us
  blocking collectives  477 us (98%)
  other arithmetic  5.75 us (1%)
    pmax x2, blocking collectives, log_totals(): top = jnp.maximum(lax.pmax(jnp.max(score, axis=0), 'adv'), rlog)  225 us
    psum x2, blocking collectives, log_totals(): total = lax.psum(jnp.sum(jnp.exp(score - top[None, :]), axis=0), 'adv')  217 us
    psum x2, blocking collectives, update_pace(): spend = lax.psum(partial_value, 'imp')  35.8 us

commit v1 on v0

v1 whole, which is shorter than its diff:
```python
import jax
import jax.numpy as jnp
from jax import lax
from jax.sharding import PartitionSpec as P

ROUNDS = 2


EPS = 0.015
NEAR = 4


def lse_of(x):
    top = jnp.max(x, axis=0)
    return top + jnp.log(jnp.sum(jnp.exp(x - top[None]), axis=0))


def on_device(far, near, groups_near, groups_far, values, limits, start_pace, reserve):
    pace = start_pace
    rlog = reserve / EPS
    prices = jnp.zeros_like(reserve)
    imp = lax.axis_size("imp")
    for step in range(ROUNDS):
        bid = pace[:, None] * values.astype(jnp.float32)
        score = bid / EPS
        own = lse_of(score)
        plane = lax.all_gather(own, "adv", axis_index_groups=groups_near)
        own = lse_of(plane)
        all_z = lax.all_to_all(
            jnp.broadcast_to(own, (far, own.shape[0])), "adv", 0, 0, axis_index_groups=groups_far, tiled=True
        )
        lse = lse_of(jnp.concatenate([all_z, rlog[None]], axis=0))
        prices = EPS * lse
        part = jnp.sum(jnp.exp(score - lse[None, :]) * bid, axis=1)
        parts = lax.all_to_all(jnp.broadcast_to(part, (imp, part.shape[0])), "imp", 0, 0, tiled=True)
        spend = jnp.sum(parts, axis=0)
        pace = jnp.minimum(1.0, pace * jnp.sqrt(limits / spend))
    return (pace, prices)


def solution(mesh):
    placed = (P("adv", "imp"), P("adv"), P("adv"), P("imp"))
    near = NEAR
    far = mesh.shape["adv"] // near
    groups_near = [[near * z + k for k in range(near)] for z in range(far)]
    groups_far = [[near * z + k for z in range(far)] for k in range(near)]

    def step(*args):
        return on_device(far, near, groups_near, groups_far, *args)

    return jax.shard_map(
        step, mesh=mesh, in_specs=placed, out_specs=(P("adv"), P("imp")), check_vma=False
    )
```

time: 487 us -> 90.7 us (0.19)
  the two profiles are of different devices: /device:TPU:1 before, /device:TPU:32 now
where the time goes in v1:
time: 90.7 us; the launch traced here: 90.4 us
  blocking collectives  83 us (92%)
  other arithmetic  6.21 us (7%)
    all_to_all x2, blocking collectives, on_device(): lax.all_to_all(jnp.broadcast_to(own, (far, own.shape[0])), 'adv', 0, 0, a...  48.2 us
    all_to_all x2, blocking collectives, on_device(): lax.all_to_all(jnp.broadcast_to(part, (imp, part.shape[0])), 'imp', 0, 0,...  24.5 us
    all_gather x2, blocking collectives, on_device(): plane = lax.all_gather(own, 'adv', axis_index_groups=groups_near)  10.4 us
    reduce_max x7, other arithmetic, lse_of(): top = jnp.max(x, axis=0)  2.25 us

profile of v1, /device:TPU:32, one launch (start us, length us, event | category | flops | bytes accessed | tf_op | source)
XLA Modules:
  0.0 90.4 jit_solution(12983010928957686713)
XLA Ops:
  0.6 0.0 copy-start
  0.6 0.0 copy-start.2
  0.6 1.7 %fusion.4 = f32[2048]{0:T(1024)S(1)} fusion(bf16[256,2048]{1,0:T(8,128)(2,1)} %param.4, f32[256]{0:T(256)} %param.6), kind=kLoop, calls=%fused_computation.6 | loop fusion | flops 2095104 | bytes 1057792 | tf_op jit(solution)/shard_map/reduce_max | solution.py:14
  2.3 0.0 copy-done
  2.3 0.0 copy-done.2
  2.3 0.0 copy-start.1
  2.4 0.6 fusion.15
  2.9 5.2 %all-gather = f32[8192]{0:T(1024)S(1)} all-gather(f32[2048]{0:T(1024)S(1)} %log_add_fusion.5), channel_id=2, replica_groups={{0,8,16,24},{32,40,48,56},{64,72,80,88},{96,104,112,120},{128,136,144,1..., dimensions={0}, use_global_device_ids=true | all-gather | bytes 40960 | tf_op jit(solution)/shard_map/all_gather | solution.py:27
  8.2 0.0 copy-start.3
  8.2 0.1 broadcast_in_dim.10
  8.3 29.4 %all_to_all.30 = f32[16,1,2048]{2,1,0:T(1,128)S(1)} all-to-all(f32[16,1,2048]{2,1,0:T(1,128)S(1)} %broadcast_in_dim.10), channel_id=1, replica_groups={{0,32,64,96,128,160,192,224,256,288,320,352,384,416,448,480},{8,40,72,1..., dimensions={0} | all-to-all | bytes 262144 | tf_op jit(solution)/shard_map/all_to_all | solution.py:29
  37.7 0.1 reduce_max.68
  37.8 0.0 copy-done.1
  37.8 0.1 fusion.20
  37.9 0.7 fusion.17
  38.6 14.4 %all_to_all.31 = f32[8,1,256]{2,1,0:T(1,128)S(1)} all-to-all(f32[8,1,256]{2,1,0:T(1,128)S(1)} %broadcast_in_dim.12), channel_id=1, replica_groups=mesh['adv'=64,'imp'=8] {'imp'}, dimensions={0} | all-to-all | bytes 16384 | tf_op jit(solution)/shard_map/all_to_all | solution.py:35
  53.1 0.0 copy-done.3
  53.1 0.4 fusion.9
  53.4 0.6 fusion.11
  54.0 5.2 %all-gather.1 = f32[8192]{0:T(1024)S(1)} all-gather(f32[2048]{0:T(1024)S(1)} %log_add_fusion.2), channel_id=3, replica_groups={{0,8,16,24},{32,40,48,56},{64,72,80,88},{96,104,112,120},{128,136,144,1..., dimensions={0}, use_global_device_ids=true | all-gather | bytes 40960 | tf_op jit(solution)/shard_map/all_gather | solution.py:27
  59.3 0.1 broadcast_in_dim.13
  59.4 18.8 %all_to_all.32 = f32[16,1,2048]{2,1,0:T(1,128)S(1)} all-to-all(f32[16,1,2048]{2,1,0:T(1,128)S(1)} %broadcast_in_dim.13), channel_id=1, replica_groups={{0,32,64,96,128,160,192,224,256,288,320,352,384,416,448,480},{8,40,72,1..., dimensions={0} | all-to-all | bytes 262144 | tf_op jit(solution)/shard_map/all_to_all | solution.py:29
  78.2 0.1 reduce_max.72
  78.4 0.1 fusion.23
  78.4 0.6 broadcast_multiply_fusion
  79.1 0.7 fusion.13
  79.8 10.0 %all_to_all.33 = f32[8,1,256]{2,1,0:T(1,128)S(1)} all-to-all(f32[8,1,256]{2,1,0:T(1,128)S(1)} %broadcast_in_dim.14), channel_id=1, replica_groups=mesh['adv'=64,'imp'=8] {'imp'}, dimensions={0} | all-to-all | bytes 16384 | tf_op jit(solution)/shard_map/all_to_all | solution.py:35
  89.8 0.6 multiply_minimum_fusion
  (20 shorter events, 0.4 us)
Async XLA Ops:
  0.6 1.7 %copy-start = (bf16[256,2048]{1,0:T(8,128)(2,1)S(1)}, bf16[256,2048]{1,0:T(8,128)(2,1)}, u32[]{:S(2)}) copy-start(bf16[256,2048]{1,0:T(8,128)(2,1)} %param.4) | copy-start | bytes 3145732
  0.6 1.7 %copy-start.2 = (f32[256]{0:T(256)S(1)}, f32[256]{0:T(256)}, u32[]{:S(2)}) copy-start(f32[256]{0:T(256)} %param.6) | copy-start | bytes 3076
  2.3 35.4 %copy-start.1 = (f32[2048]{0:T(1024)S(1)}, f32[2048]{0:T(1024)}, u32[]{:S(2)}) copy-start(f32[2048]{0:T(1024)} %param.7) | copy-start | bytes 24580
  8.2 44.8 %copy-start.3 = (f32[256]{0:T(256)S(1)}, f32[256]{0:T(256)}, u32[]{:S(2)}) copy-start(f32[256]{0:T(256)} %param.5) | copy-start | bytes 3076

commit v2 on v1

v2 whole, which is shorter than its diff:
```python
import math

import jax
import jax.numpy as jnp
from jax import lax
from jax.experimental import pallas as pl
from jax.experimental.pallas import tpu as pltpu
from jax.sharding import PartitionSpec as P

EPS = 0.015
NEAR = 4
LANES = 128
CHUNKS = 4
UNIT = math.log2(math.e) / EPS
BACK = EPS / math.log2(math.e)
LOG2E = math.log2(math.e)

VMEM = pl.BlockSpec(memory_space=pltpu.VMEM)
HBM = pl.BlockSpec(memory_space=pltpu.HBM)


def log2(x):
    return jnp.log(x) * LOG2E


def spread_rows(scale_ref, pace, rows):
    for h in range(rows // LANES):
        row = jnp.broadcast_to(pace[h : h + 1, :] * UNIT, (LANES, LANES))
        scale_ref[pl.ds(h * LANES, LANES), :] = row.T


def strip_lse(s, v, scale_ref, lse_ref, top_ref, weighted_ref):
    y = v.astype(jnp.float32) * scale_ref[...]
    top = jnp.max(y, axis=0, keepdims=True)
    e = jnp.exp2(y - top)
    weighted_ref[:, pl.ds(s * LANES, LANES)] = y * e
    top_ref[pl.ds(s, 1), :] = top
    lse_ref[pl.ds(s, 1), :] = top + log2(jnp.sum(e, axis=0, keepdims=True))


def first_kernel(
    values_hbm, pace_hbm, limits_hbm, reserve_hbm,
    lse_ref, top_ref, weighted_ref, values_ref, pace_ref, limits_ref, reserve_ref,
    scale_ref, sems,
):
    rows, columns = values_ref.shape
    width = columns // CHUNKS
    small = []
    for n, (source, target) in enumerate(
        ((pace_hbm, pace_ref), (limits_hbm, limits_ref), (reserve_hbm, reserve_ref))
    ):
        small.append(pltpu.make_async_copy(source, target, sems.at[CHUNKS + n]))
    small[0].start()
    copies = []
    for c in range(CHUNKS):
        part = pl.ds(c * width, width)
        copies.append(pltpu.make_async_copy(values_hbm.at[:, part], values_ref.at[:, part], sems.at[c]))
        copies[c].start()
    small[1].start()
    small[2].start()
    small[0].wait()
    spread_rows(scale_ref, pace_ref[...], rows)
    per = width // LANES
    for c in range(CHUNKS):
        copies[c].wait()
        for s in range(c * per, (c + 1) * per):
            strip_lse(s, values_ref[:, pl.ds(s * LANES, LANES)], scale_ref, lse_ref, top_ref, weighted_ref)
    small[1].wait()
    small[2].wait()


def new_pace(parts, pace, limits):
    spend = jnp.sum(parts, axis=0) * BACK
    return jnp.minimum(1.0, pace * jnp.sqrt(limits / spend))


def next_kernel(values_ref, parts_ref, pace_ref, limits_ref, pace_out, lse_ref, top_ref, weighted_ref, scale_ref):
    rows, columns = values_ref.shape
    pace = new_pace(parts_ref[...], pace_ref[...], limits_ref[...])
    pace_out[...] = pace
    spread_rows(scale_ref, pace, rows)
    for s in range(columns // LANES):
        strip_lse(s, values_ref[:, pl.ds(s * LANES, LANES)], scale_ref, lse_ref, top_ref, weighted_ref)


def shares(z_ref, reserve_ref, top_ref, weighted_ref, parts_ref):
    rlog = reserve_ref[...] * UNIT
    peak = jnp.maximum(jnp.max(z_ref[...], axis=0), rlog)
    total = jnp.sum(jnp.exp2(z_ref[...] - peak[None]), axis=0) + jnp.exp2(rlog - peak)
    lse = peak + log2(total)
    w = jnp.exp2(top_ref[...] - lse)
    rows, columns = weighted_ref.shape
    acc = weighted_ref[:, pl.ds(0, LANES)] * w[0:1, :]
    for s in range(1, columns // LANES):
        acc = acc + weighted_ref[:, pl.ds(s * LANES, LANES)] * w[s : s + 1, :]
    for h in range(rows // LANES):
        part = jnp.sum(acc[h * LANES : (h + 1) * LANES, :].T, axis=0, keepdims=True)
        parts_ref[:, pl.ds(h, 1), :] = jnp.broadcast_to(part[None], (parts_ref.shape[0], 1, LANES))
    return lse


def spend_kernel(z_ref, reserve_ref, top_ref, weighted_ref, parts_ref):
    shares(z_ref, reserve_ref, top_ref, weighted_ref, parts_ref)


def last_spend_kernel(z_ref, reserve_ref, top_ref, weighted_ref, parts_ref, prices_ref):
    prices_ref[...] = BACK * shares(z_ref, reserve_ref, top_ref, weighted_ref, parts_ref)


PARAMS = pltpu.CompilerParams(vmem_limit_bytes=16 * 2**20)


def f32(*shape):
    return jax.ShapeDtypeStruct(shape, jnp.float32)


def on_device(far, near, groups_near, groups_far, values, limits, start_pace, reserve):
    rows, columns = values.shape
    imp = lax.axis_size("imp")
    strips, halves = columns // LANES, rows // LANES
    limits = limits.reshape(halves, LANES)
    pace = start_pace.reshape(halves, LANES)
    reserve = reserve.reshape(strips, LANES)
    row_lse = (f32(strips, LANES), f32(strips, LANES), f32(rows, columns))

    def to_all_z(own):
        plane = lax.all_gather(own, "adv", axis_index_groups=groups_near)
        peak = jnp.max(plane, axis=0)
        own = peak + log2(jnp.sum(jnp.exp2(plane - peak[None]), axis=0))
        return lax.all_to_all(
            jnp.broadcast_to(own[None], (far, strips, LANES)), "adv", 0, 0, axis_index_groups=groups_far, tiled=True
        )

    own, top, weighted, values, pace, limits, reserve = pl.pallas_call(
        first_kernel,
        compiler_params=PARAMS,
        out_shape=row_lse
        + (jax.ShapeDtypeStruct((rows, columns), values.dtype), f32(halves, LANES), f32(halves, LANES), f32(strips, LANES)),
        in_specs=[HBM] * 4,
        out_specs=(VMEM,) * 7,
        scratch_shapes=[
            pltpu.VMEM((rows, LANES), jnp.float32),
            pltpu.SemaphoreType.DMA((CHUNKS + 3,)),
        ],
    )(*(pltpu.with_memory_space_constraint(a, pltpu.HBM) for a in (values, pace, limits, reserve)))
    parts = pl.pallas_call(
        spend_kernel,
        compiler_params=PARAMS,
        out_shape=f32(imp, halves, LANES),
        in_specs=[VMEM] * 4,
        out_specs=VMEM,
    )(to_all_z(own), reserve, top, weighted)
    parts = lax.all_to_all(parts, "imp", 0, 0, tiled=True)
    pace, own, top, weighted = pl.pallas_call(
        next_kernel,
        compiler_params=PARAMS,
        out_shape=(f32(halves, LANES),) + row_lse,
        in_specs=[VMEM] * 4,
        out_specs=(VMEM,) * 4,
        scratch_shapes=[pltpu.VMEM((rows, LANES), jnp.float32)],
    )(values, parts, pace, limits)
    parts, prices = pl.pallas_call(
        last_spend_kernel,
        compiler_params=PARAMS,
        out_shape=(f32(imp, halves, LANES), f32(strips, LANES)),
        in_specs=[VMEM] * 4,
        out_specs=(VMEM, VMEM),
    )(to_all_z(own), reserve, top, weighted)
    parts = lax.all_to_all(parts, "imp", 0, 0, tiled=True)
    pace = new_pace(parts, pace, limits)
    return (pace.reshape(rows), prices.reshape(columns))


def solution(mesh):
    placed = (P("adv", "imp"), P("adv"), P("adv"), P("imp"))
    near = NEAR
    far = mesh.shape["adv"] // near
    groups_near = [[near * z + k for k in range(near)] for z in range(far)]
    groups_far = [[near * z + k for z in range(far)] for k in range(near)]

    def step(*args):
        return on_device(far, near, groups_near, groups_far, *args)

    return jax.shard_map(
        step, mesh=mesh, in_specs=placed, out_specs=(P("adv"), P("imp")), check_vma=False
    )
```

time: 90.7 us -> 88.4 us (0.975)
  other arithmetic: 6.21 us -> 0.67 us
  Pallas kernels: 0 us -> 3.66 us
    pallas_call x0 -> x4, Pallas kernels: none -> 3.66 us  [the longest x1 1.85 us: on_device(): pl.pallas_call(first_kernel, compiler_params=PARAMS, out_shape=row_lse +...]
    reduce_sum x10 -> x3, other arithmetic: 2.72 us -> 0.06 us  [the longest x2 0.04 us: to_all_z(): own = peak + log2(jnp.sum(jnp.exp2(plane - peak[None]), axis=0))]
    reduce_max x7 -> x2, other arithmetic: 2.25 us -> 0.01 us  [to_all_z(): peak = jnp.max(plane, axis=0)]
where the time goes in v2:
time: 88.4 us; the launch traced here: 88.1 us
  blocking collectives  83 us (94%)
  Pallas kernels  3.66 us (4%)
    all_to_all x2, blocking collectives, to_all_z(): lax.all_to_all(jnp.broadcast_to(own[None], (far, strips, LANES)), 'adv',...  48.2 us
    all_to_all x2, blocking collectives, on_device(): parts = lax.all_to_all(parts, 'imp', 0, 0, tiled=True)  24.4 us
    all_gather x2, blocking collectives, to_all_z(): plane = lax.all_gather(own, 'adv', axis_index_groups=groups_near)  10.4 us
    pallas_call x1, Pallas kernels, on_device(): pl.pallas_call(first_kernel, compiler_params=PARAMS, out_shape=row_lse +...  1.85 us

profile of v2, /device:TPU:32, one launch (start us, length us, event | category | flops | bytes accessed | tf_op | source)
XLA Modules:
  0.0 88.1 jit_solution(18391452669592269411)
XLA Ops:
  0.6 1.8 %shard_map.59 = (f32[16,128]{1,0:T(8,128)S(1)}, f32[16,128]{1,0:T(8,128)S(1)}, f32[256,2048]{1,0:T(8,128)S(1)}, bf16[256,2048]{1,0:T(8,128)(2,1)S(1)}, f32[2,128...) custom-call(bf16[256,2048]{1,0:T(8,128)(2,1)} %values_hbm.1, f32[2,128]{1,0:T(2,128)} %bitcast.13, ...), custom_call_target="tpu_custom_call" | custom-call | tf_op jit(solution)/shard_map/pallas_call | solution.py:134
  2.5 5.2 %all-gather = f32[64,128]{1,0:T(8,128)S(1)} all-gather(f32[16,128]{1,0:T(8,128)S(1)} %get-tuple-element.16), channel_id=2, replica_groups={{0,8,16,24},{32,40,48,56},{64,72,80,88},{96,104,112,120},{128,136,144,1..., dimensions={0}, use_global_device_ids=true | all-gather | bytes 40960 | tf_op jit(solution)/shard_map/all_gather | solution.py:127
  7.7 29.4 %all_to_all.20.z_ref = f32[16,16,128]{2,1,0:T(8,128)S(1)} all-to-all(f32[16,16,128]{2,1,0:T(8,128)S(1)} %broadcast_in_dim.4), channel_id=1, replica_groups={{0,32,64,96,128,160,192,224,256,288,320,352,384,416,448,480},{8,40,72,1..., dimensions={0} | all-to-all | bytes 262144 | tf_op jit(solution)/shard_map/all_to_all | solution.py:130
  37.1 0.3 shard_map.60
  37.4 14.4 %all_to_all.21.parts_ref = f32[8,2,128]{2,1,0:T(2,128)S(1)} all-to-all(f32[8,2,128]{2,1,0:T(2,128)S(1)} %shard_map.60), channel_id=1, replica_groups=mesh['adv'=64,'imp'=8] {'imp'}, dimensions={0} | all-to-all | bytes 16384 | tf_op jit(solution)/shard_map/all_to_all | solution.py:153
  51.8 0.8 shard_map.61
  52.6 5.2 %all-gather.1 = f32[64,128]{1,0:T(8,128)S(1)} all-gather(f32[16,128]{1,0:T(8,128)S(1)} %get-tuple-element.23), channel_id=3, replica_groups={{0,8,16,24},{32,40,48,56},{64,72,80,88},{96,104,112,120},{128,136,144,1..., dimensions={0}, use_global_device_ids=true | all-gather | bytes 40960 | tf_op jit(solution)/shard_map/all_gather | solution.py:127
  57.8 18.8 %all_to_all.22.z_ref = f32[16,16,128]{2,1,0:T(8,128)S(1)} all-to-all(f32[16,16,128]{2,1,0:T(8,128)S(1)} %broadcast_in_dim.5), channel_id=1, replica_groups={{0,32,64,96,128,160,192,224,256,288,320,352,384,416,448,480},{8,40,72,1..., dimensions={0} | all-to-all | bytes 262144 | tf_op jit(solution)/shard_map/all_to_all | solution.py:130
  76.7 0.8 shard_map.62
  77.4 10.0 %all_to_all.23 = f32[8,2,128]{2,1,0:T(2,128)S(1)} all-to-all(f32[8,2,128]{2,1,0:T(2,128)S(1)} %get-tuple-element.26), channel_id=1, replica_groups=mesh['adv'=64,'imp'=8] {'imp'}, dimensions={0} | all-to-all | bytes 16384 | tf_op jit(solution)/shard_map/all_to_all | solution.py:169
  87.5 0.6 minimum_bitcast_fusion
  (9 shorter events, 0.1 us)

commit v3 on v2

v3 whole, which is shorter than its diff:
```python
import math

import jax
import jax.numpy as jnp
from jax import lax
from jax.experimental import pallas as pl
from jax.experimental.pallas import tpu as pltpu
from jax.sharding import PartitionSpec as P

EPS = 0.015
CORES = 2
NEAR = 4
LANES = 128
CHUNKS = 4
UNIT = math.log2(math.e) / EPS
BACK = EPS / math.log2(math.e)
LOG2E = math.log2(math.e)

VMEM = pl.BlockSpec(memory_space=pltpu.VMEM)
HBM = pl.BlockSpec(memory_space=pltpu.HBM)
PARAMS = pltpu.CompilerParams(vmem_limit_bytes=16 * 2**20)


def log2(x):
    return jnp.log(x) * LOG2E


def join(x):
    peak = jnp.max(x, axis=0)
    return peak + log2(jnp.sum(jnp.exp2(x - peak[None]), axis=0))


def join_kernel(x_ref, out_ref):
    strips = out_ref.shape[-2]
    out_ref[...] = jnp.broadcast_to(join(x_ref[:, pl.ds(0, strips), :]), out_ref.shape)


def joined(x, *shape):
    return pl.pallas_call(
        join_kernel,
        compiler_params=PARAMS,
        out_shape=jax.ShapeDtypeStruct(shape, jnp.float32),
        in_specs=[VMEM],
        out_specs=VMEM,
    )(x)


def strip(s):
    return pl.ds(s * LANES, LANES)


def spread_rows(scale_ref, pace):
    for h in range(scale_ref.shape[0] // LANES):
        row = jnp.broadcast_to(pace[h : h + 1, :] * UNIT, (LANES, LANES))
        scale_ref[strip(h), :] = row.T


def strip_lse(s, v, scale_ref, weighted_ref):
    y = v.astype(jnp.float32) * scale_ref[...]
    top = jnp.max(y, axis=0, keepdims=True)
    e = jnp.exp2(y - top)
    weighted_ref[:, strip(s)] = y * e
    return top, top + log2(jnp.sum(e, axis=0, keepdims=True))


def first_kernel(
    values_hbm, pace_hbm, limits_hbm, reserve_hbm,
    send_ref, top_ref, weighted_ref, values_ref, wide_ref, reserve_ref,
    pace_ref, limits_ref, scale_ref, sems,
):
    rows, columns = values_ref.shape
    strips, halves = columns // LANES, rows // LANES
    width = columns // CHUNKS
    pairs = ((pace_hbm, pace_ref), (limits_hbm, limits_ref), (reserve_hbm, reserve_ref))
    small = [pltpu.make_async_copy(a, b, sems.at[CHUNKS + n]) for n, (a, b) in enumerate(pairs)]
    small[0].start()
    copies = []
    for c in range(CHUNKS):
        part = pl.ds(c * width, width)
        copies.append(pltpu.make_async_copy(values_hbm.at[:, part], values_ref.at[:, part], sems.at[c]))
        copies[c].start()
    small[1].start()
    small[2].start()
    small[0].wait()
    send_ref[pl.ds(strips, halves), :] = pace_ref[...]
    spread_rows(scale_ref, pace_ref[...])
    per = width // LANES
    for c in range(CHUNKS):
        copies[c].wait()
        for s in range(c * per, (c + 1) * per):
            v = values_ref[:, strip(s)].astype(jnp.float32)
            wide_ref[:, strip(s)] = v
            top, lse = strip_lse(s, v, scale_ref, weighted_ref)
            top_ref[pl.ds(s, 1), :] = top
            send_ref[pl.ds(s, 1), :] = lse
    small[1].wait()
    send_ref[pl.ds(strips + halves, halves), :] = limits_ref[...]
    send_ref[pl.ds(strips + 2 * halves, 4), :] = jnp.zeros((4, LANES), jnp.float32)
    small[2].wait()


def new_pace(parts, pace, limits):
    spend = jnp.sum(parts, axis=0) * BACK
    return jnp.minimum(1.0, pace * jnp.sqrt(limits / spend))


def next_kernel(
    values_ref, other_ref, parts_ref, send_ref, pair_ref,
    pace_out, limits_out, lse_ref, top_ref, weighted_ref, scale_ref,
):
    rows, columns = values_ref.shape
    strips, halves = columns // LANES, rows // LANES
    both = 2 * halves
    mine = send_ref[pl.ds(strips, both), :]
    theirs = pair_ref[0, pl.ds(strips, both), :]
    pace = jnp.concatenate([mine[:halves], theirs[:halves]], axis=0)
    limits = jnp.concatenate([mine[halves:], theirs[halves:]], axis=0)
    pace = new_pace(parts_ref[...], pace, limits)
    pace_out[...] = pace
    limits_out[...] = limits
    ends = []
    for k, source in enumerate((values_ref, other_ref)):
        block = pl.ds(k * rows, rows)
        spread_rows(scale_ref.at[block], pace[k * halves : (k + 1) * halves])
    for s in range(strips):
        for k, source in enumerate((values_ref, other_ref)):
            block = pl.ds(k * rows, rows)
            top, lse = strip_lse(s, source[:, strip(s)], scale_ref.at[block], weighted_ref.at[block])
            top_ref[k, pl.ds(s, 1), :] = top
            ends.append(lse)
        one, two = ends[-2:]
        peak = jnp.maximum(one, two)
        lse_ref[pl.ds(s, 1), :] = peak + log2(jnp.exp2(one - peak) + jnp.exp2(two - peak))


def total_lse(z_ref, reserve_ref):
    rlog = reserve_ref[...] * UNIT
    peak = jnp.maximum(jnp.max(z_ref[...], axis=0), rlog)
    total = jnp.sum(jnp.exp2(z_ref[...] - peak[None]), axis=0) + jnp.exp2(rlog - peak)
    return peak + log2(total)


def put_parts(parts_ref, first, acc):
    for h in range(acc.shape[0] // LANES):
        part = jnp.sum(acc[h * LANES : (h + 1) * LANES, :].T, axis=0, keepdims=True)
        parts_ref[:, pl.ds(first + h, 1), :] = jnp.broadcast_to(part[None], (parts_ref.shape[0], 1, LANES))


def weighted_sums(weighted_ref, block, w):
    acc = weighted_ref[block, strip(0)] * w[0:1, :]
    for s in range(1, w.shape[0]):
        acc = acc + weighted_ref[block, strip(s)] * w[s : s + 1, :]
    return acc


def spend_kernel(z_ref, reserve_ref, top_ref, weighted_ref, other_ref, pair_ref, parts_ref, scale_ref):
    rows, columns = weighted_ref.shape
    strips, halves = columns // LANES, rows // LANES
    lse = total_lse(z_ref, reserve_ref)
    spread_rows(scale_ref, pair_ref[0, pl.ds(strips, halves), :])
    put_parts(parts_ref, 0, weighted_sums(weighted_ref, pl.ds(0, rows), jnp.exp2(top_ref[...] - lse)))
    for h in range(halves):
        acc = jnp.zeros((LANES, LANES), jnp.float32)
        for s in range(strips):
            y = other_ref[strip(h), strip(s)] * scale_ref[strip(h), :]
            acc = acc + y * jnp.exp2(y - lse[s : s + 1, :])
        put_parts(parts_ref, halves + h, acc)


def last_spend_kernel(z_ref, reserve_ref, top_ref, weighted_ref, parts_ref, prices_ref):
    rows = weighted_ref.shape[0] // 2
    lse = total_lse(z_ref, reserve_ref)
    prices_ref[...] = BACK * lse
    for k in range(2):
        w = jnp.exp2(top_ref[k] - lse)
        put_parts(parts_ref, k * (rows // LANES), weighted_sums(weighted_ref, pl.ds(k * rows, rows), w))


def f32(*shape):
    return jax.ShapeDtypeStruct(shape, jnp.float32)


def on_device(groups, values, limits, start_pace, reserve):
    rows, columns = values.shape
    imp = lax.axis_size("imp")
    far = lax.axis_size("adv") // NEAR
    strips, halves = columns // LANES, rows // LANES
    both = 2 * halves
    args = (values, start_pace.reshape(halves, LANES), limits.reshape(halves, LANES), reserve.reshape(strips, LANES))
    args = [pltpu.with_memory_space_constraint(a, pltpu.HBM) for a in args]

    def along_z(own):
        own = joined(lax.all_gather(own, "adv", axis_index_groups=groups["chips"]), far, strips, LANES)
        return lax.all_to_all(own, ("adv", "imp"), 0, 0, axis_index_groups=groups["z"], tiled=True)

    send, top, weighted, values, wide, reserve = pl.pallas_call(
        first_kernel,
        compiler_params=PARAMS,
        out_shape=(
            f32(strips + 2 * halves + 4, LANES),
            f32(strips, LANES),
            f32(rows, columns),
            jax.ShapeDtypeStruct((rows, columns), values.dtype),
            f32(rows, columns),
            f32(strips, LANES),
        ),
        in_specs=[HBM] * 4,
        out_specs=(VMEM,) * 6,
        scratch_shapes=[
            pltpu.VMEM((halves, LANES), jnp.float32),
            pltpu.VMEM((halves, LANES), jnp.float32),
            pltpu.VMEM((rows, LANES), jnp.float32),
            pltpu.SemaphoreType.DMA((CHUNKS + 3,)),
        ],
    )(*args)
    pair = lax.all_gather(send, "adv", axis_index_groups=groups["cores"])
    wide, pair = lax.optimization_barrier((wide, pair))
    other = lax.ppermute(wide, "adv", groups["ship"])
    parts = pl.pallas_call(
        spend_kernel,
        compiler_params=PARAMS,
        out_shape=f32(imp, both, LANES),
        in_specs=[VMEM] * 6,
        out_specs=VMEM,
        scratch_shapes=[pltpu.VMEM((rows, LANES), jnp.float32)],
    )(along_z(joined(pair, strips, LANES)), reserve, top, weighted, other, pair)
    parts = lax.all_to_all(parts, "imp", 0, 0, tiled=True)
    pace, limits, own, top, weighted = pl.pallas_call(
        next_kernel,
        compiler_params=PARAMS,
        out_shape=(
            f32(both, LANES),
            f32(both, LANES),
            f32(strips, LANES),
            f32(2, strips, LANES),
            f32(2 * rows, columns),
        ),
        in_specs=[VMEM] * 5,
        out_specs=(VMEM,) * 5,
        scratch_shapes=[pltpu.VMEM((2 * rows, LANES), jnp.float32)],
    )(values, other, parts, send, pair)
    parts, prices = pl.pallas_call(
        last_spend_kernel,
        compiler_params=PARAMS,
        out_shape=(f32(imp, both, LANES), f32(strips, LANES)),
        in_specs=[VMEM] * 4,
        out_specs=(VMEM, VMEM),
    )(along_z(own), reserve, top, weighted)
    parts = lax.all_to_all(parts, "imp", 0, 0, tiled=True)
    pace = new_pace(parts, pace, limits)
    done = jnp.concatenate([prices, pace, jnp.zeros((8 - both, LANES), jnp.float32)], axis=0)
    done = lax.all_gather(done, "adv", axis_index_groups=groups["cores"])[1]
    mine = done[strips : strips + halves]
    theirs = done[strips + halves : strips + both]
    pace = jnp.where(lax.axis_index("adv") % CORES == 1, mine, theirs)
    return (pace.reshape(rows), done[:strips].reshape(columns))


def solution(mesh):
    placed = (P("adv", "imp"), P("adv"), P("adv"), P("imp"))
    adv, imp = mesh.shape["adv"], mesh.shape["imp"]
    far, chips = adv // NEAR, NEAR // CORES

    def at(z, chip, core):
        return z * NEAR + chip * CORES + core

    along_z = [[at(z, c, 1) * imp + i for z in range(far)] for c in range(chips) for i in range(imp)]
    plane = [at(z, c, 0) * imp + i for z in range(far) for c in range(chips) for i in range(imp)]
    groups = dict(
        cores=[[at(z, c, k) for k in range(CORES)] for z in range(far) for c in range(chips)],
        chips=[[at(z, c, k) for c in range(chips)] for z in range(far) for k in range(CORES)],
        ship=[(at(z, c, 0), at(z, c, 1)) for z in range(far) for c in range(chips)],
        z=along_z + [plane[n : n + far] for n in range(0, len(plane), far)],
    )

    def step(*args):
        return on_device(groups, *args)

    return jax.shard_map(
        step, mesh=mesh, in_specs=placed, out_specs=(P("adv"), P("imp")), check_vma=False
    )
```

time: 88.4 us -> 85 us (0.962)
  the two profiles are of different devices: /device:TPU:32 before, /device:TPU:1 now
where the time goes in v3:
time: 85 us; the launch traced here: 84.6 us
  blocking collectives  66.4 us (78%)
  waiting for transfers between devices  6.38 us (8%)
  Pallas kernels  5.2 us (6%)
  starting transfers between devices  4.59 us (5%)
    all_to_all x2, blocking collectives, along_z(): lax.all_to_all(own, ('adv', 'imp'), 0, 0, axis_index_groups=groups['z'],...  36.6 us
    all_to_all x1, blocking collectives, on_device(): parts = lax.all_to_all(parts, 'imp', 0, 0, tiled=True)  13 us
    all_gather x1, blocking collectives, on_device(): pair = lax.all_gather(send, 'adv', axis_index_groups=groups['cores'])  8.32 us
    all_gather x2, blocking collectives, along_z(): lax.all_gather(own, 'adv', axis_index_groups=groups['chips'])  6.67 us
    all_to_all x1, waiting for transfers between devices, on_device(): parts = lax.all_to_all(parts, 'imp', 0, 0, tiled=True)  6.37 us
    all_to_all x1, starting transfers between devices, on_device(): parts = lax.all_to_all(parts, 'imp', 0, 0, tiled=True)  3.31 us
    pallas_call x1, Pallas kernels, on_device(): pl.pallas_call(first_kernel, compiler_params=PARAMS, out_shape=(f32(strip...  2 us
    all_gather x1, blocking collectives, on_device(): done = lax.all_gather(done, 'adv', axis_index_groups=groups['cores'])[1]  1.82 us
  transfers between devices with their start and end apart: 2, of which 1 were waited for; matrix products, arithmetic and copies ran while one was open for 0% of the time, Pallas kernels for 0%

profile of v3, /device:TPU:1, one launch (start us, length us, event | category | flops | bytes accessed | tf_op | source)
XLA Modules:
  0.0 84.6 jit_solution(4686236591652912356)
XLA Ops:
  0.6 2.0 %shard_map.59 = (f32[24,128]{1,0:T(8,128)S(1)}, f32[16,128]{1,0:T(8,128)S(1)}, f32[256,2048]{1,0:T(8,128)S(1)}, bf16[256,2048]{1,0:T(8,128)(2,1)S(1)}, f32[256,2048]{1,0:T(8,128)S(1)}, /*index=5*/f32[16,128]{1,0:T(8,128)S(1)}) custom-call(bf16[256,2048]{1,0:T(8,128)(2,1)} %values_hbm.1, f32[2,128]{1,0:T(2,128)} %bitcast.19, f32[2,128]{1,0:T(2,128)} %bitcast.20, ...), custom_call_target="tpu_custom_call" | custom-call | tf_op jit(solution)/shard_map/pallas_call | solution.py:196
  2.6 8.3 %all-gather = f32[48,128]{1,0:T(8,128)S(1)} all-gather(f32[24,128]{1,0:T(8,128)S(1)} %get-tuple-element.19.send_ref), channel_id=2, replica_groups={{0,8},{16,24},{32,40},{48,56},{64,72},{80,88},{96,104},{112,120},{128,1..., dimensions={0}, use_global_device_ids=true | all-gather | bytes 36864 | tf_op jit(solution)/shard_map/all_gather | solution.py:216
  11.0 1.3 %collective-permute-start = (f32[256,2048]{1,0:T(8,128)S(1)}, f32[256,2048]{1,0:T(8,128)S(1)}, u32[]{:S(2)}, u32[]{:S(2)}) collective-permute-start(f32[256,2048]{1,0:T(8,128)S(1)} %get-tuple-element.20), channel_id=1, source_target_pairs={{0,8},{16,24},{32,40},{48,56},{64,72},{80,88},{96,104},{112,120},{... | collective-permute-start | bytes 6291464 | tf_op jit(solution)/shard_map/ppermute | solution.py:218
  12.3 3.2 %all-gather.1 = f32[32,128]{1,0:T(8,128)S(1)} all-gather(f32[16,128]{1,0:T(8,128)S(1)} %shard_map.60), channel_id=3, replica_groups={{0,16},{8,24},{32,48},{40,56},{64,80},{72,88},{96,112},{104,120},{128,1..., dimensions={0}, use_global_device_ids=true | all-gather | bytes 24576 | tf_op jit(solution)/shard_map/all_gather | solution.py:193
  15.5 21.3 %all_to_all.20.z_ref = f32[16,16,128]{2,1,0:T(8,128)S(1)} all-to-all(f32[16,16,128]{2,1,0:T(8,128)S(1)} %shard_map.61), channel_id=1, replica_groups={{8,40,72,104,136,168,200,232,264,296,328,360,392,424,456,488},{9,41,73,..., dimensions={0} | all-to-all | bytes 262144 | tf_op jit(solution)/shard_map/all_to_all | solution.py:194
  36.8 0.0 collective-permute-done.other_ref
  36.8 0.6 shard_map.62
  37.4 13.0 %all_to_all.21.parts_ref = f32[8,4,128]{2,1,0:T(4,128)S(1)} all-to-all(f32[8,4,128]{2,1,0:T(4,128)S(1)} %shard_map.62), channel_id=1, replica_groups=mesh['adv'=64,'imp'=8] {'imp'}, dimensions={0} | all-to-all | bytes 32768 | tf_op jit(solution)/shard_map/all_to_all | solution.py:227
  50.4 1.5 %shard_map.63 = (f32[4,128]{1,0:T(4,128)S(1)}, f32[4,128]{1,0:T(4,128)S(1)}, f32[16,128]{1,0:T(8,128)S(1)}, f32[2,16,128]{2,1,0:T(8,128)S(1)}, f32[512,2048]{1,0:T(8,128)S(1)}) custom-call(bf16[256,2048]{1,0:T(8,128)(2,1)S(1)} %get-tuple-element.17.values_ref, f32[256,2048]{1,0:T(8,128)S(1)} %collective-permute-done.other_ref, ...), custom_call_target="tpu_custom_call" | custom-call | tf_op jit(solution)/shard_map/pallas_call | solution.py:228
  52.0 3.5 %all-gather.2 = f32[32,128]{1,0:T(8,128)S(1)} all-gather(f32[16,128]{1,0:T(8,128)S(1)} %get-tuple-element.25), channel_id=4, replica_groups={{0,16},{8,24},{32,48},{40,56},{64,80},{72,88},{96,112},{104,120},{128,1..., dimensions={0}, use_global_device_ids=true | all-gather | bytes 24576 | tf_op jit(solution)/shard_map/all_gather | solution.py:193
  55.5 15.3 %all_to_all.22.z_ref = f32[16,16,128]{2,1,0:T(8,128)S(1)} all-to-all(f32[16,16,128]{2,1,0:T(8,128)S(1)} %shard_map.64), channel_id=1, replica_groups={{8,40,72,104,136,168,200,232,264,296,328,360,392,424,456,488},{9,41,73,..., dimensions={0} | all-to-all | bytes 262144 | tf_op jit(solution)/shard_map/all_to_all | solution.py:194
  70.7 1.0 %shard_map.65 = (f32[8,4,128]{2,1,0:T(4,128)}, f32[16,128]{1,0:T(8,128)S(1)}) custom-call(f32[16,16,128]{2,1,0:T(8,128)S(1)} %all_to_all.22.z_ref, f32[16,128]{1,0:T(8,128)S(1)} %get-tuple-element.22.reserve_ref, f32[2,16,128]{2,1,0:T(8,128)S(1)} %get-tuple-element.26.top_ref, f32[512,2048]{1,0:T(8,128)S(1)} %get-tuple-element.27.weighted_ref), custom_call_target="tpu_custom_call" | custom-call | tf_op jit(solution)/shard_map/pallas_call | solution.py:242
  71.7 3.3 %all-to-all-start.3 = ((f32[8,4,128]{2,1,0:T(4,128)}), f32[8,4,128]{2,1,0:T(4,128)S(1)}, u32[]{:S(2)}, u32[]{:S(2)}) async-start(f32[8,4,128]{2,1,0:T(4,128)} %get-tuple-element.31), calls=%async_computation.3 | async-start | bytes 32768 | tf_op jit(solution)/shard_map/all_to_all | solution.py:249
  75.1 0.1 pad.2.clone
  75.1 6.4 %all-to-all-done.3 = f32[8,4,128]{2,1,0:T(4,128)S(1)} async-done(((f32[8,4,128]{2,1,0:T(4,128)}), f32[8,4,128]{2,1,0:T(4,128)S(1)}, u32[]{:S(2)}, u32[]{:S(2)}) %all-to-all-start.3) | async-done | bytes 16416 | tf_op jit(solution)/shard_map/all_to_all | solution.py:249
  81.6 0.1 maximum_maximum_fusion
  81.6 1.8 %all-gather.3 = f32[48,128]{1,0:T(8,128)S(1)} all-gather(f32[24,128]{1,0:T(8,128)S(1)} %maximum_maximum_fusion), channel_id=5, replica_groups={{0,8},{16,24},{32,40},{48,56},{64,72},{80,88},{96,104},{112,120},{128,1..., dimensions={0}, use_global_device_ids=true | all-gather | bytes 36864 | tf_op jit(solution)/shard_map/all_gather | solution.py:252
  83.4 0.6 slice_bitcast_fusion
  84.0 0.6 fusion
  (6 shorter events, 0.1 us)
Async XLA Ops:
  11.0 25.9 %collective-permute-start = (f32[256,2048]{1,0:T(8,128)S(1)}, f32[256,2048]{1,0:T(8,128)S(1)}, u32[]{:S(2)}, u32[]{:S(2)}) collective-permute-start(f32[256,2048]{1,0:T(8,128)S(1)} %get-tuple-element.20), channel_id=1, source_target_pairs={{0,8},{16,24},{32,40},{48,56},{64,72},{80,88},{96,104},{112,120},{... | collective-permute-start | bytes 6291464 | tf_op jit(solution)/shard_map/ppermute | solution.py:218
  71.7 9.8 %all-to-all-start.3 = ((f32[8,4,128]{2,1,0:T(4,128)}), f32[8,4,128]{2,1,0:T(4,128)S(1)}, u32[]{:S(2)}, u32[]{:S(2)}) async-start(f32[8,4,128]{2,1,0:T(4,128)} %get-tuple-element.31), calls=%async_computation.3 | async-start | bytes 32768 | tf_op jit(solution)/shard_map/all_to_all | solution.py:249

commit v4 on v3

--- a/solution.py
+++ b/solution.py
@@ -176,6 +176,22 @@
         put_parts(parts_ref, k * (rows // LANES), weighted_sums(weighted_ref, pl.ds(k * rows, rows), w))
 
 
+def pack_kernel(parts_ref, pace_ref, limits_ref, prices_ref, out_ref):
+    strips, both = prices_ref.shape[0], pace_ref.shape[0]
+    out_ref[pl.ds(0, strips), :] = prices_ref[...]
+    out_ref[pl.ds(strips, both), :] = new_pace(parts_ref[...], pace_ref[...], limits_ref[...])
+    out_ref[pl.ds(strips + both, 8 - both), :] = jnp.zeros((8 - both, LANES), jnp.float32)
+
+
+def pick_kernel(pair_ref, pace_ref, prices_ref):
+    strips, halves = prices_ref.shape[0], pace_ref.shape[0]
+    prices_ref[...] = pair_ref[1, pl.ds(0, strips), :]
+    second = lax.axis_index("adv") % CORES == 1
+    mine = pair_ref[1, pl.ds(strips, halves), :]
+    theirs = pair_ref[1, pl.ds(strips + halves, halves), :]
+    pace_ref[...] = jnp.where(second, mine, theirs)
+
+
 def f32(*shape):
     return jax.ShapeDtypeStruct(shape, jnp.float32)
 
@@ -247,13 +263,21 @@
         out_specs=(VMEM, VMEM),
     )(along_z(own), reserve, top, weighted)
     parts = lax.all_to_all(parts, "imp", 0, 0, tiled=True)
-    pace = new_pace(parts, pace, limits)
-    done = jnp.concatenate([prices, pace, jnp.zeros((8 - both, LANES), jnp.float32)], axis=0)
-    done = lax.all_gather(done, "adv", axis_index_groups=groups["cores"])[1]
-    mine = done[strips : strips + halves]
-    theirs = done[strips + halves : strips + both]
-    pace = jnp.where(lax.axis_index("adv") % CORES == 1, mine, theirs)
-    return (pace.reshape(rows), done[:strips].reshape(columns))
+    done = pl.pallas_call(
+        pack_kernel,
+        compiler_params=PARAMS,
+        out_shape=f32(strips + 8, LANES),
+        in_specs=[VMEM] * 4,
+        out_specs=VMEM,
+    )(parts, pace, limits, prices)
+    pace, prices = pl.pallas_call(
+        pick_kernel,
+        compiler_params=PARAMS,
+        out_shape=(f32(halves, LANES), f32(strips, LANES)),
+        in_specs=[VMEM],
+        out_specs=(VMEM, VMEM),
+    )(lax.all_gather(done, "adv", axis_index_groups=groups["cores"]))
+    return (pace.reshape(rows), prices.reshape(columns))
 
 
 def solution(mesh):

time: 85 us -> 82.8 us (0.974)
  blocking collectives: 66.4 us -> 75.3 us
  waiting for transfers between devices: 6.38 us -> 0.01 us
  starting transfers between devices: 4.59 us -> 1.28 us
    all_to_all x1 -> x2, blocking collectives: 13 us -> 21.9 us  [on_device(): parts = lax.all_to_all(parts, 'imp', 0, 0, tiled=True)]
    all_to_all x1 -> x0, waiting for transfers between devices: 6.37 us -> none  [on_device(): parts = lax.all_to_all(parts, 'imp', 0, 0, tiled=True)]
    all_to_all x1 -> x0, starting transfers between devices: 3.31 us -> none  [on_device(): parts = lax.all_to_all(parts, 'imp', 0, 0, tiled=True)]
  transfers between devices with their start and end apart: 2 -> 1, of which waited for: 1 -> 0; matrix products, arithmetic and copies ran while one was open for 0% -> 0% of each run, Pallas kernels for 0% -> 0%
where the time goes in v4:
time: 82.8 us; the launch traced here: 82.5 us
  blocking collectives  75.3 us (91%)
  Pallas kernels  5.22 us (6%)
  starting transfers between devices  1.28 us (2%)
    all_to_all x2, blocking collectives, along_z(): lax.all_to_all(own, ('adv', 'imp'), 0, 0, axis_index_groups=groups['z'],...  36.6 us
    all_to_all x2, blocking collectives, on_device(): parts = lax.all_to_all(parts, 'imp', 0, 0, tiled=True)  21.9 us
    all_gather x1, blocking collectives, on_device(): pair = lax.all_gather(send, 'adv', axis_index_groups=groups['cores'])  8.32 us
    all_gather x2, blocking collectives, along_z(): lax.all_gather(own, 'adv', axis_index_groups=groups['chips'])  6.67 us
    pallas_call x1, Pallas kernels, on_device(): pl.pallas_call(first_kernel, compiler_params=PARAMS, out_shape=(f32(strip...  2 us
    all_gather x1, blocking collectives, on_device(): lax.all_gather(done, 'adv', axis_index_groups=groups['cores'])  1.82 us
  transfers between devices with their start and end apart: 1, of which 0 were waited for; matrix products, arithmetic and copies ran while one was open for 0% of the time, Pallas kernels for 0%

profile of v4, /device:TPU:1, one launch (start us, length us, event | category | flops | bytes accessed | tf_op | source)
XLA Modules:
  0.0 82.5 jit_solution(161221603765320457)
XLA Ops:
  0.6 2.0 %shard_map.59 = (f32[24,128]{1,0:T(8,128)S(1)}, f32[16,128]{1,0:T(8,128)S(1)}, f32[256,2048]{1,0:T(8,128)S(1)}, bf16[256,2048]{1,0:T(8,128)(2,1)S(1)}, f32[256,2048]{1,0:T(8,128)S(1)}, /*index=5*/f32[16,128]{1,0:T(8,128)S(1)}) custom-call(bf16[256,2048]{1,0:T(8,128)(2,1)} %values_hbm.1, f32[2,128]{1,0:T(2,128)} %bitcast.16, f32[2,128]{1,0:T(2,128)} %bitcast.17, ...), custom_call_target="tpu_custom_call" | custom-call | tf_op jit(solution)/shard_map/pallas_call | solution.py:212
  2.6 8.3 %all-gather = f32[48,128]{1,0:T(8,128)S(1)} all-gather(f32[24,128]{1,0:T(8,128)S(1)} %get-tuple-element.21.send_ref), channel_id=2, replica_groups={{0,8},{16,24},{32,40},{48,56},{64,72},{80,88},{96,104},{112,120},{128,1..., dimensions={0}, use_global_device_ids=true | all-gather | bytes 36864 | tf_op jit(solution)/shard_map/all_gather | solution.py:232
  11.0 1.3 %collective-permute-start = (f32[256,2048]{1,0:T(8,128)S(1)}, f32[256,2048]{1,0:T(8,128)S(1)}, u32[]{:S(2)}, u32[]{:S(2)}) collective-permute-start(f32[256,2048]{1,0:T(8,128)S(1)} %get-tuple-element.22), channel_id=1, source_target_pairs={{0,8},{16,24},{32,40},{48,56},{64,72},{80,88},{96,104},{112,120},{... | collective-permute-start | bytes 6291464 | tf_op jit(solution)/shard_map/ppermute | solution.py:234
  12.3 3.2 %all-gather.1 = f32[32,128]{1,0:T(8,128)S(1)} all-gather(f32[16,128]{1,0:T(8,128)S(1)} %shard_map.60), channel_id=3, replica_groups={{0,16},{8,24},{32,48},{40,56},{64,80},{72,88},{96,112},{104,120},{128,1..., dimensions={0}, use_global_device_ids=true | all-gather | bytes 24576 | tf_op jit(solution)/shard_map/all_gather | solution.py:209
  15.5 21.3 %all_to_all.20.z_ref = f32[16,16,128]{2,1,0:T(8,128)S(1)} all-to-all(f32[16,16,128]{2,1,0:T(8,128)S(1)} %shard_map.61), channel_id=1, replica_groups={{8,40,72,104,136,168,200,232,264,296,328,360,392,424,456,488},{9,41,73,..., dimensions={0} | all-to-all | bytes 262144 | tf_op jit(solution)/shard_map/all_to_all | solution.py:210
  36.8 0.0 collective-permute-done.other_ref
  36.8 0.6 shard_map.62
  37.4 13.0 %all_to_all.21.parts_ref = f32[8,4,128]{2,1,0:T(4,128)S(1)} all-to-all(f32[8,4,128]{2,1,0:T(4,128)S(1)} %shard_map.62), channel_id=1, replica_groups=mesh['adv'=64,'imp'=8] {'imp'}, dimensions={0} | all-to-all | bytes 32768 | tf_op jit(solution)/shard_map/all_to_all | solution.py:243
  50.4 1.5 %shard_map.63 = (f32[4,128]{1,0:T(4,128)S(1)}, f32[4,128]{1,0:T(4,128)S(1)}, f32[16,128]{1,0:T(8,128)S(1)}, f32[2,16,128]{2,1,0:T(8,128)S(1)}, f32[512,2048]{1,0:T(8,128)S(1)}) custom-call(bf16[256,2048]{1,0:T(8,128)(2,1)S(1)} %get-tuple-element.19.values_ref, f32[256,2048]{1,0:T(8,128)S(1)} %collective-permute-done.other_ref, ...), custom_call_target="tpu_custom_call" | custom-call | tf_op jit(solution)/shard_map/pallas_call | solution.py:244
  52.0 3.5 %all-gather.2 = f32[32,128]{1,0:T(8,128)S(1)} all-gather(f32[16,128]{1,0:T(8,128)S(1)} %get-tuple-element.27), channel_id=4, replica_groups={{0,16},{8,24},{32,48},{40,56},{64,80},{72,88},{96,112},{104,120},{128,1..., dimensions={0}, use_global_device_ids=true | all-gather | bytes 24576 | tf_op jit(solution)/shard_map/all_gather | solution.py:209
  55.5 15.3 %all_to_all.22.z_ref = f32[16,16,128]{2,1,0:T(8,128)S(1)} all-to-all(f32[16,16,128]{2,1,0:T(8,128)S(1)} %shard_map.64), channel_id=1, replica_groups={{8,40,72,104,136,168,200,232,264,296,328,360,392,424,456,488},{9,41,73,..., dimensions={0} | all-to-all | bytes 262144 | tf_op jit(solution)/shard_map/all_to_all | solution.py:210
  70.7 0.4 shard_map.65
  71.1 8.9 %all_to_all.23.parts_ref = f32[8,4,128]{2,1,0:T(4,128)S(1)} all-to-all(f32[8,4,128]{2,1,0:T(4,128)S(1)} %get-tuple-element.30), channel_id=1, replica_groups=mesh['adv'=64,'imp'=8] {'imp'}, dimensions={0} | all-to-all | bytes 32768 | tf_op jit(solution)/shard_map/all_to_all | solution.py:265
  80.1 1.8 %all-gather.3 = f32[48,128]{1,0:T(8,128)S(1)} all-gather(f32[24,128]{1,0:T(8,128)S(1)} %shard_map.66), channel_id=5, replica_groups={{0,8},{16,24},{32,40},{48,56},{64,72},{80,88},{96,104},{112,120},{128,1..., dimensions={0}, use_global_device_ids=true | all-gather | bytes 36864 | tf_op jit(solution)/shard_map/all_gather | solution.py:279
  81.9 0.6 shard_map.67
  (4 shorter events, 0.1 us)
Async XLA Ops:
  11.0 25.9 %collective-permute-start = (f32[256,2048]{1,0:T(8,128)S(1)}, f32[256,2048]{1,0:T(8,128)S(1)}, u32[]{:S(2)}, u32[]{:S(2)}) collective-permute-start(f32[256,2048]{1,0:T(8,128)S(1)} %get-tuple-element.22), channel_id=1, source_target_pairs={{0,8},{16,24},{32,40},{48,56},{64,72},{80,88},{96,104},{112,120},{... | collective-permute-start | bytes 6291464 | tf_op jit(solution)/shard_map/ppermute | solution.py:234

commit v5 on v4

--- a/solution.py
+++ b/solution.py
@@ -12,6 +12,8 @@
 NEAR = 4
 LANES = 128
 CHUNKS = 4
+FIRST_Z = 9
+FIRST_IMP = 5
 UNIT = math.log2(math.e) / EPS
 BACK = EPS / math.log2(math.e)
 LOG2E = math.log2(math.e)
@@ -240,7 +242,7 @@
         out_specs=VMEM,
         scratch_shapes=[pltpu.VMEM((rows, LANES), jnp.float32)],
     )(along_z(joined(pair, strips, LANES)), reserve, top, weighted, other, pair)
-    parts = lax.all_to_all(parts, "imp", 0, 0, tiled=True)
+    parts = lax.all_to_all(parts, "imp", 0, 0, axis_index_groups=groups["imp"], tiled=True)
     pace, limits, own, top, weighted = pl.pallas_call(
         next_kernel,
         compiler_params=PARAMS,
@@ -262,7 +264,7 @@
         in_specs=[VMEM] * 4,
         out_specs=(VMEM, VMEM),
     )(along_z(own), reserve, top, weighted)
-    parts = lax.all_to_all(parts, "imp", 0, 0, tiled=True)
+    parts = lax.all_to_all(parts, "imp", 0, 0, axis_index_groups=groups["imp"], tiled=True)
     done = pl.pallas_call(
         pack_kernel,
         compiler_params=PARAMS,
@@ -288,12 +290,14 @@
     def at(z, chip, core):
         return z * NEAR + chip * CORES + core
 
-    along_z = [[at(z, c, 1) * imp + i for z in range(far)] for c in range(chips) for i in range(imp)]
+    order = [(z + FIRST_Z) % far for z in range(far)]
+    along_z = [[at(z, c, 1) * imp + i for z in order] for c in range(chips) for i in range(imp)]
     plane = [at(z, c, 0) * imp + i for z in range(far) for c in range(chips) for i in range(imp)]
     groups = dict(
         cores=[[at(z, c, k) for k in range(CORES)] for z in range(far) for c in range(chips)],
         chips=[[at(z, c, k) for c in range(chips)] for z in range(far) for k in range(CORES)],
         ship=[(at(z, c, 0), at(z, c, 1)) for z in range(far) for c in range(chips)],
+        imp=[[(i + FIRST_IMP) % imp for i in range(imp)]],
         z=along_z + [plane[n : n + far] for n in range(0, len(plane), far)],
     )
 

time: 82.8 us -> 74.8 us (0.903)
  blocking collectives: 75.3 us -> 67.3 us
    all_to_all x2, blocking collectives: 21.9 us -> 18 us  [on_device(): lax.all_to_all(parts, 'imp', 0, 0, axis_index_groups=groups['imp'], tiled...]
    all_to_all x2, blocking collectives: 36.6 us -> 32.7 us  [along_z(): lax.all_to_all(own, ('adv', 'imp'), 0, 0, axis_index_groups=groups['z'],...]
where the time goes in v5:
time: 74.8 us; the launch traced here: 74.5 us
  blocking collectives  67.3 us (90%)
  Pallas kernels  5.22 us (7%)
  starting transfers between devices  1.28 us (2%)
    all_to_all x2, blocking collectives, along_z(): lax.all_to_all(own, ('adv', 'imp'), 0, 0, axis_index_groups=groups['z'],...  32.7 us
    all_to_all x2, blocking collectives, on_device(): lax.all_to_all(parts, 'imp', 0, 0, axis_index_groups=groups['imp'], tiled...  18 us
    all_gather x1, blocking collectives, on_device(): pair = lax.all_gather(send, 'adv', axis_index_groups=groups['cores'])  8.32 us
    all_gather x2, blocking collectives, along_z(): lax.all_gather(own, 'adv', axis_index_groups=groups['chips'])  6.42 us
    pallas_call x1, Pallas kernels, on_device(): pl.pallas_call(first_kernel, compiler_params=PARAMS, out_shape=(f32(strip...  2 us
    all_gather x1, blocking collectives, on_device(): lax.all_gather(done, 'adv', axis_index_groups=groups['cores'])  1.82 us
    pallas_call x1, Pallas kernels, on_device(): pl.pallas_call(next_kernel, compiler_params=PARAMS, out_shape=(f32(both,...  1.54 us
  transfers between devices with their start and end apart: 1, of which 0 were waited for; matrix products, arithmetic and copies ran while one was open for 0% of the time, Pallas kernels for 0%

profile of v5, /device:TPU:1, one launch (start us, length us, event | category | flops | bytes accessed | tf_op | source)
XLA Modules:
  0.0 74.5 jit_solution(10485650216738400941)
XLA Ops:
  0.6 2.0 %shard_map.59 = (f32[24,128]{1,0:T(8,128)S(1)}, f32[16,128]{1,0:T(8,128)S(1)}, f32[256,2048]{1,0:T(8,128)S(1)}, bf16[256,2048]{1,0:T(8,128)(2,1)S(1)}, f32[256,2048]{1,0:T(8,128)S(1)}, /*index=5*/f32[16,128]{1,0:T(8,128)S(1)}) custom-call(bf16[256,2048]{1,0:T(8,128)(2,1)} %values_hbm.1, f32[2,128]{1,0:T(2,128)} %bitcast.16, f32[2,128]{1,0:T(2,128)} %bitcast.17, ...), custom_call_target="tpu_custom_call" | custom-call | tf_op jit(solution)/shard_map/pallas_call | solution.py:214
  2.6 8.3 %all-gather = f32[48,128]{1,0:T(8,128)S(1)} all-gather(f32[24,128]{1,0:T(8,128)S(1)} %get-tuple-element.21.send_ref), channel_id=2, replica_groups={{0,8},{16,24},{32,40},{48,56},{64,72},{80,88},{96,104},{112,120},{128,1..., dimensions={0}, use_global_device_ids=true | all-gather | bytes 36864 | tf_op jit(solution)/shard_map/all_gather | solution.py:234
  11.0 1.3 %collective-permute-start = (f32[256,2048]{1,0:T(8,128)S(1)}, f32[256,2048]{1,0:T(8,128)S(1)}, u32[]{:S(2)}, u32[]{:S(2)}) collective-permute-start(f32[256,2048]{1,0:T(8,128)S(1)} %get-tuple-element.22), channel_id=1, source_target_pairs={{0,8},{16,24},{32,40},{48,56},{64,72},{80,88},{96,104},{112,120},{... | collective-permute-start | bytes 6291464 | tf_op jit(solution)/shard_map/ppermute | solution.py:236
  12.3 3.2 %all-gather.1 = f32[32,128]{1,0:T(8,128)S(1)} all-gather(f32[16,128]{1,0:T(8,128)S(1)} %shard_map.60), channel_id=3, replica_groups={{0,16},{8,24},{32,48},{40,56},{64,80},{72,88},{96,112},{104,120},{128,1..., dimensions={0}, use_global_device_ids=true | all-gather | bytes 24576 | tf_op jit(solution)/shard_map/all_gather | solution.py:211
  15.5 17.0 %all_to_all.20.z_ref = f32[16,16,128]{2,1,0:T(8,128)S(1)} all-to-all(f32[16,16,128]{2,1,0:T(8,128)S(1)} %shard_map.61), channel_id=1, replica_groups={{296,328,360,392,424,456,488,8,40,72,104,136,168,200,232,264},{297,329,..., dimensions={0} | all-to-all | bytes 262144 | tf_op jit(solution)/shard_map/all_to_all | solution.py:212
  32.5 0.0 collective-permute-done.other_ref
  32.5 0.6 shard_map.62
  33.1 9.3 %all_to_all.21.parts_ref = f32[8,4,128]{2,1,0:T(4,128)S(1)} all-to-all(f32[8,4,128]{2,1,0:T(4,128)S(1)} %shard_map.62), channel_id=1, replica_groups={{5,6,7,0,1,2,3,4},{13,14,15,8,9,10,11,12},{21,22,23,16,17,18,19,20},{29..., dimensions={0} | all-to-all | bytes 32768 | tf_op jit(solution)/shard_map/all_to_all | solution.py:245
  42.4 1.5 %shard_map.63 = (f32[4,128]{1,0:T(4,128)S(1)}, f32[4,128]{1,0:T(4,128)S(1)}, f32[16,128]{1,0:T(8,128)S(1)}, f32[2,16,128]{2,1,0:T(8,128)S(1)}, f32[512,2048]{1,0:T(8,128)S(1)}) custom-call(bf16[256,2048]{1,0:T(8,128)(2,1)S(1)} %get-tuple-element.19.values_ref, f32[256,2048]{1,0:T(8,128)S(1)} %collective-permute-done.other_ref, ...), custom_call_target="tpu_custom_call" | custom-call | tf_op jit(solution)/shard_map/pallas_call | solution.py:246
  43.9 3.2 %all-gather.2 = f32[32,128]{1,0:T(8,128)S(1)} all-gather(f32[16,128]{1,0:T(8,128)S(1)} %get-tuple-element.27), channel_id=4, replica_groups={{0,16},{8,24},{32,48},{40,56},{64,80},{72,88},{96,112},{104,120},{128,1..., dimensions={0}, use_global_device_ids=true | all-gather | bytes 24576 | tf_op jit(solution)/shard_map/all_gather | solution.py:211
  47.1 15.7 %all_to_all.22.z_ref = f32[16,16,128]{2,1,0:T(8,128)S(1)} all-to-all(f32[16,16,128]{2,1,0:T(8,128)S(1)} %shard_map.64), channel_id=1, replica_groups={{296,328,360,392,424,456,488,8,40,72,104,136,168,200,232,264},{297,329,..., dimensions={0} | all-to-all | bytes 262144 | tf_op jit(solution)/shard_map/all_to_all | solution.py:212
  62.9 0.4 shard_map.65
  63.3 8.7 %all_to_all.23.parts_ref = f32[8,4,128]{2,1,0:T(4,128)S(1)} all-to-all(f32[8,4,128]{2,1,0:T(4,128)S(1)} %get-tuple-element.30), channel_id=1, replica_groups={{5,6,7,0,1,2,3,4},{13,14,15,8,9,10,11,12},{21,22,23,16,17,18,19,20},{29..., dimensions={0} | all-to-all | bytes 32768 | tf_op jit(solution)/shard_map/all_to_all | solution.py:267
  72.0 1.8 %all-gather.3 = f32[48,128]{1,0:T(8,128)S(1)} all-gather(f32[24,128]{1,0:T(8,128)S(1)} %shard_map.66), channel_id=5, replica_groups={{0,8},{16,24},{32,40},{48,56},{64,72},{80,88},{96,104},{112,120},{128,1..., dimensions={0}, use_global_device_ids=true | all-gather | bytes 36864 | tf_op jit(solution)/shard_map/all_gather | solution.py:281
  73.8 0.6 shard_map.67
  (4 shorter events, 0.1 us)
Async XLA Ops:
  11.0 21.5 %collective-permute-start = (f32[256,2048]{1,0:T(8,128)S(1)}, f32[256,2048]{1,0:T(8,128)S(1)}, u32[]{:S(2)}, u32[]{:S(2)}) collective-permute-start(f32[256,2048]{1,0:T(8,128)S(1)} %get-tuple-element.22), channel_id=1, source_target_pairs={{0,8},{16,24},{32,40},{48,56},{64,72},{80,88},{96,104},{112,120},{... | collective-permute-start | bytes 6291464 | tf_op jit(solution)/shard_map/ppermute | solution.py:236

commit v6 on v5

--- a/solution.py
+++ b/solution.py
@@ -12,8 +12,8 @@
 NEAR = 4
 LANES = 128
 CHUNKS = 4
-FIRST_Z = 9
-FIRST_IMP = 5
+ORDER_Z = (9, 0, 1, 2, 3, 15, 14, 4, 5, 6, 7, 13, 12, 11, 10, 8)
+ORDER_IMP = (5, 0, 2, 6, 1, 3, 7, 4)
 UNIT = math.log2(math.e) / EPS
 BACK = EPS / math.log2(math.e)
 LOG2E = math.log2(math.e)
@@ -290,14 +290,15 @@
     def at(z, chip, core):
         return z * NEAR + chip * CORES + core
 
-    order = [(z + FIRST_Z) % far for z in range(far)]
+    order = ORDER_Z if far == len(ORDER_Z) else range(far)
+    over_imp = ORDER_IMP if imp == len(ORDER_IMP) else range(imp)
     along_z = [[at(z, c, 1) * imp + i for z in order] for c in range(chips) for i in range(imp)]
     plane = [at(z, c, 0) * imp + i for z in range(far) for c in range(chips) for i in range(imp)]
     groups = dict(
         cores=[[at(z, c, k) for k in range(CORES)] for z in range(far) for c in range(chips)],
         chips=[[at(z, c, k) for c in range(chips)] for z in range(far) for k in range(CORES)],
         ship=[(at(z, c, 0), at(z, c, 1)) for z in range(far) for c in range(chips)],
-        imp=[[(i + FIRST_IMP) % imp for i in range(imp)]],
+        imp=[list(over_imp)],
         z=along_z + [plane[n : n + far] for n in range(0, len(plane), far)],
     )
 

time: 74.8 us -> 74.3 us (level)
  no operation moved by 1% of the time
where the time goes in v6:
time: 74.3 us; the launch traced here: 74 us
  blocking collectives  66.8 us (90%)
  Pallas kernels  5.22 us (7%)
  starting transfers between devices  1.28 us (2%)
    all_to_all x2, blocking collectives, along_z(): lax.all_to_all(own, ('adv', 'imp'), 0, 0, axis_index_groups=groups['z'],...  32.4 us
    all_to_all x2, blocking collectives, on_device(): lax.all_to_all(parts, 'imp', 0, 0, axis_index_groups=groups['imp'], tiled...  17.8 us
    all_gather x1, blocking collectives, on_device(): pair = lax.all_gather(send, 'adv', axis_index_groups=groups['cores'])  8.32 us
    all_gather x2, blocking collectives, along_z(): lax.all_gather(own, 'adv', axis_index_groups=groups['chips'])  6.42 us
    pallas_call x1, Pallas kernels, on_device(): pl.pallas_call(first_kernel, compiler_params=PARAMS, out_shape=(f32(strip...  2 us
    all_gather x1, blocking collectives, on_device(): lax.all_gather(done, 'adv', axis_index_groups=groups['cores'])  1.82 us
    pallas_call x1, Pallas kernels, on_device(): pl.pallas_call(next_kernel, compiler_params=PARAMS, out_shape=(f32(both,...  1.54 us
  transfers between devices with their start and end apart: 1, of which 0 were waited for; matrix products, arithmetic and copies ran while one was open for 0% of the time, Pallas kernels for 0%

profile of v6, /device:TPU:1, one launch (start us, length us, event | category | flops | bytes accessed | tf_op | source)
XLA Modules:
  0.0 74.0 jit_solution(11732321745988193568)
XLA Ops:
  0.6 2.0 %shard_map.59 = (f32[24,128]{1,0:T(8,128)S(1)}, f32[16,128]{1,0:T(8,128)S(1)}, f32[256,2048]{1,0:T(8,128)S(1)}, bf16[256,2048]{1,0:T(8,128)(2,1)S(1)}, f32[256,2048]{1,0:T(8,128)S(1)}, /*index=5*/f32[16,128]{1,0:T(8,128)S(1)}) custom-call(bf16[256,2048]{1,0:T(8,128)(2,1)} %values_hbm.1, f32[2,128]{1,0:T(2,128)} %bitcast.16, f32[2,128]{1,0:T(2,128)} %bitcast.17, ...), custom_call_target="tpu_custom_call" | custom-call | tf_op jit(solution)/shard_map/pallas_call | solution.py:214
  2.6 8.3 %all-gather = f32[48,128]{1,0:T(8,128)S(1)} all-gather(f32[24,128]{1,0:T(8,128)S(1)} %get-tuple-element.21.send_ref), channel_id=2, replica_groups={{0,8},{16,24},{32,40},{48,56},{64,72},{80,88},{96,104},{112,120},{128,1..., dimensions={0}, use_global_device_ids=true | all-gather | bytes 36864 | tf_op jit(solution)/shard_map/all_gather | solution.py:234
  11.0 1.3 %collective-permute-start = (f32[256,2048]{1,0:T(8,128)S(1)}, f32[256,2048]{1,0:T(8,128)S(1)}, u32[]{:S(2)}, u32[]{:S(2)}) collective-permute-start(f32[256,2048]{1,0:T(8,128)S(1)} %get-tuple-element.22), channel_id=1, source_target_pairs={{0,8},{16,24},{32,40},{48,56},{64,72},{80,88},{96,104},{112,120},{... | collective-permute-start | bytes 6291464 | tf_op jit(solution)/shard_map/ppermute | solution.py:236
  12.3 3.2 %all-gather.1 = f32[32,128]{1,0:T(8,128)S(1)} all-gather(f32[16,128]{1,0:T(8,128)S(1)} %shard_map.60), channel_id=3, replica_groups={{0,16},{8,24},{32,48},{40,56},{64,80},{72,88},{96,112},{104,120},{128,1..., dimensions={0}, use_global_device_ids=true | all-gather | bytes 24576 | tf_op jit(solution)/shard_map/all_gather | solution.py:211
  15.5 16.6 %all_to_all.20.z_ref = f32[16,16,128]{2,1,0:T(8,128)S(1)} all-to-all(f32[16,16,128]{2,1,0:T(8,128)S(1)} %shard_map.61), channel_id=1, replica_groups={{296,8,40,72,104,488,456,136,168,200,232,424,392,360,328,264},{297,9,41..., dimensions={0} | all-to-all | bytes 262144 | tf_op jit(solution)/shard_map/all_to_all | solution.py:212
  32.1 0.0 collective-permute-done.other_ref
  32.1 0.6 shard_map.62
  32.7 9.2 %all_to_all.21.parts_ref = f32[8,4,128]{2,1,0:T(4,128)S(1)} all-to-all(f32[8,4,128]{2,1,0:T(4,128)S(1)} %shard_map.62), channel_id=1, replica_groups={{5,0,2,6,1,3,7,4},{13,8,10,14,9,11,15,12},{21,16,18,22,17,19,23,20},{29..., dimensions={0} | all-to-all | bytes 32768 | tf_op jit(solution)/shard_map/all_to_all | solution.py:245
  42.0 1.5 %shard_map.63 = (f32[4,128]{1,0:T(4,128)S(1)}, f32[4,128]{1,0:T(4,128)S(1)}, f32[16,128]{1,0:T(8,128)S(1)}, f32[2,16,128]{2,1,0:T(8,128)S(1)}, f32[512,2048]{1,0:T(8,128)S(1)}) custom-call(bf16[256,2048]{1,0:T(8,128)(2,1)S(1)} %get-tuple-element.19.values_ref, f32[256,2048]{1,0:T(8,128)S(1)} %collective-permute-done.other_ref, ...), custom_call_target="tpu_custom_call" | custom-call | tf_op jit(solution)/shard_map/pallas_call | solution.py:246
  43.5 3.2 %all-gather.2 = f32[32,128]{1,0:T(8,128)S(1)} all-gather(f32[16,128]{1,0:T(8,128)S(1)} %get-tuple-element.27), channel_id=4, replica_groups={{0,16},{8,24},{32,48},{40,56},{64,80},{72,88},{96,112},{104,120},{128,1..., dimensions={0}, use_global_device_ids=true | all-gather | bytes 24576 | tf_op jit(solution)/shard_map/all_gather | solution.py:211
  46.8 15.8 %all_to_all.22.z_ref = f32[16,16,128]{2,1,0:T(8,128)S(1)} all-to-all(f32[16,16,128]{2,1,0:T(8,128)S(1)} %shard_map.64), channel_id=1, replica_groups={{296,8,40,72,104,488,456,136,168,200,232,424,392,360,328,264},{297,9,41..., dimensions={0} | all-to-all | bytes 262144 | tf_op jit(solution)/shard_map/all_to_all | solution.py:212
  62.5 0.4 shard_map.65
  63.0 8.6 %all_to_all.23.parts_ref = f32[8,4,128]{2,1,0:T(4,128)S(1)} all-to-all(f32[8,4,128]{2,1,0:T(4,128)S(1)} %get-tuple-element.30), channel_id=1, replica_groups={{5,0,2,6,1,3,7,4},{13,8,10,14,9,11,15,12},{21,16,18,22,17,19,23,20},{29..., dimensions={0} | all-to-all | bytes 32768 | tf_op jit(solution)/shard_map/all_to_all | solution.py:267
  71.6 1.8 %all-gather.3 = f32[48,128]{1,0:T(8,128)S(1)} all-gather(f32[24,128]{1,0:T(8,128)S(1)} %shard_map.66), channel_id=5, replica_groups={{0,8},{16,24},{32,40},{48,56},{64,72},{80,88},{96,104},{112,120},{128,1..., dimensions={0}, use_global_device_ids=true | all-gather | bytes 36864 | tf_op jit(solution)/shard_map/all_gather | solution.py:281
  73.4 0.6 shard_map.67
  (4 shorter events, 0.1 us)
Async XLA Ops:
  11.0 21.2 %collective-permute-start = (f32[256,2048]{1,0:T(8,128)S(1)}, f32[256,2048]{1,0:T(8,128)S(1)}, u32[]{:S(2)}, u32[]{:S(2)}) collective-permute-start(f32[256,2048]{1,0:T(8,128)S(1)} %get-tuple-element.22), channel_id=1, source_target_pairs={{0,8},{16,24},{32,40},{48,56},{64,72},{80,88},{96,104},{112,120},{... | collective-permute-start | bytes 6291464 | tf_op jit(solution)/shard_map/ppermute | solution.py:236

commit v7 on v6

--- a/solution.py
+++ b/solution.py
@@ -114,7 +114,7 @@
     strips, halves = columns // LANES, rows // LANES
     both = 2 * halves
     mine = send_ref[pl.ds(strips, both), :]
-    theirs = pair_ref[0, pl.ds(strips, both), :]
+    theirs = pair_ref[1, pl.ds(strips, both), :]
     pace = jnp.concatenate([mine[:halves], theirs[:halves]], axis=0)
     limits = jnp.concatenate([mine[halves:], theirs[halves:]], axis=0)
     pace = new_pace(parts_ref[...], pace, limits)
@@ -159,7 +159,7 @@
     rows, columns = weighted_ref.shape
     strips, halves = columns // LANES, rows // LANES
     lse = total_lse(z_ref, reserve_ref)
-    spread_rows(scale_ref, pair_ref[0, pl.ds(strips, halves), :])
+    spread_rows(scale_ref, pair_ref[1, pl.ds(strips, halves), :])
     put_parts(parts_ref, 0, weighted_sums(weighted_ref, pl.ds(0, rows), jnp.exp2(top_ref[...] - lse)))
     for h in range(halves):
         acc = jnp.zeros((LANES, LANES), jnp.float32)
@@ -187,10 +187,10 @@
 
 def pick_kernel(pair_ref, pace_ref, prices_ref):
     strips, halves = prices_ref.shape[0], pace_ref.shape[0]
-    prices_ref[...] = pair_ref[1, pl.ds(0, strips), :]
+    prices_ref[...] = pair_ref[0, pl.ds(0, strips), :]
     second = lax.axis_index("adv") % CORES == 1
-    mine = pair_ref[1, pl.ds(strips, halves), :]
-    theirs = pair_ref[1, pl.ds(strips + halves, halves), :]
+    mine = pair_ref[0, pl.ds(strips, halves), :]
+    theirs = pair_ref[0, pl.ds(strips + halves, halves), :]
     pace_ref[...] = jnp.where(second, mine, theirs)
 
 
@@ -295,7 +295,7 @@
     along_z = [[at(z, c, 1) * imp + i for z in order] for c in range(chips) for i in range(imp)]
     plane = [at(z, c, 0) * imp + i for z in range(far) for c in range(chips) for i in range(imp)]
     groups = dict(
-        cores=[[at(z, c, k) for k in range(CORES)] for z in range(far) for c in range(chips)],
+        cores=[[at(z, c, k) for k in reversed(range(CORES))] for z in range(far) for c in range(chips)],
         chips=[[at(z, c, k) for c in range(chips)] for z in range(far) for k in range(CORES)],
         ship=[(at(z, c, 0), at(z, c, 1)) for z in range(far) for c in range(chips)],
         imp=[list(over_imp)],

time: 74.3 us -> 74.3 us (level)
  no operation moved by 1% of the time
where the time goes in v7:
time: 74.3 us; the launch traced here: 74 us
  blocking collectives  66.8 us (90%)
  Pallas kernels  5.22 us (7%)
  starting transfers between devices  1.28 us (2%)
    all_to_all x2, blocking collectives, along_z(): lax.all_to_all(own, ('adv', 'imp'), 0, 0, axis_index_groups=groups['z'],...  32.4 us
    all_to_all x2, blocking collectives, on_device(): lax.all_to_all(parts, 'imp', 0, 0, axis_index_groups=groups['imp'], tiled...  17.8 us
    all_gather x1, blocking collectives, on_device(): pair = lax.all_gather(send, 'adv', axis_index_groups=groups['cores'])  8.32 us
    all_gather x2, blocking collectives, along_z(): lax.all_gather(own, 'adv', axis_index_groups=groups['chips'])  6.42 us
    pallas_call x1, Pallas kernels, on_device(): pl.pallas_call(first_kernel, compiler_params=PARAMS, out_shape=(f32(strip...  2 us
    all_gather x1, blocking collectives, on_device(): lax.all_gather(done, 'adv', axis_index_groups=groups['cores'])  1.82 us
    pallas_call x1, Pallas kernels, on_device(): pl.pallas_call(next_kernel, compiler_params=PARAMS, out_shape=(f32(both,...  1.54 us
  transfers between devices with their start and end apart: 1, of which 0 were waited for; matrix products, arithmetic and copies ran while one was open for 0% of the time, Pallas kernels for 0%

profile of v7, /device:TPU:1, one launch (start us, length us, event | category | flops | bytes accessed | tf_op | source)
XLA Modules:
  0.0 74.0 jit_solution(2090557030202218007)
XLA Ops:
  0.6 2.0 %shard_map.59 = (f32[24,128]{1,0:T(8,128)S(1)}, f32[16,128]{1,0:T(8,128)S(1)}, f32[256,2048]{1,0:T(8,128)S(1)}, bf16[256,2048]{1,0:T(8,128)(2,1)S(1)}, f32[256,2048]{1,0:T(8,128)S(1)}, /*index=5*/f32[16,128]{1,0:T(8,128)S(1)}) custom-call(bf16[256,2048]{1,0:T(8,128)(2,1)} %values_hbm.1, f32[2,128]{1,0:T(2,128)} %bitcast.16, f32[2,128]{1,0:T(2,128)} %bitcast.17, ...), custom_call_target="tpu_custom_call" | custom-call | tf_op jit(solution)/shard_map/pallas_call | solution.py:214
  2.6 8.3 %all-gather = f32[48,128]{1,0:T(8,128)S(1)} all-gather(f32[24,128]{1,0:T(8,128)S(1)} %get-tuple-element.21.send_ref), channel_id=2, replica_groups={{8,0},{24,16},{40,32},{56,48},{72,64},{88,80},{104,96},{120,112},{136,1..., dimensions={0}, use_global_device_ids=true | all-gather | bytes 36864 | tf_op jit(solution)/shard_map/all_gather | solution.py:234
  11.0 1.3 %collective-permute-start = (f32[256,2048]{1,0:T(8,128)S(1)}, f32[256,2048]{1,0:T(8,128)S(1)}, u32[]{:S(2)}, u32[]{:S(2)}) collective-permute-start(f32[256,2048]{1,0:T(8,128)S(1)} %get-tuple-element.22), channel_id=1, source_target_pairs={{0,8},{16,24},{32,40},{48,56},{64,72},{80,88},{96,104},{112,120},{... | collective-permute-start | bytes 6291464 | tf_op jit(solution)/shard_map/ppermute | solution.py:236
  12.3 3.2 %all-gather.1 = f32[32,128]{1,0:T(8,128)S(1)} all-gather(f32[16,128]{1,0:T(8,128)S(1)} %shard_map.60), channel_id=3, replica_groups={{0,16},{8,24},{32,48},{40,56},{64,80},{72,88},{96,112},{104,120},{128,1..., dimensions={0}, use_global_device_ids=true | all-gather | bytes 24576 | tf_op jit(solution)/shard_map/all_gather | solution.py:211
  15.5 16.6 %all_to_all.20.z_ref = f32[16,16,128]{2,1,0:T(8,128)S(1)} all-to-all(f32[16,16,128]{2,1,0:T(8,128)S(1)} %shard_map.61), channel_id=1, replica_groups={{296,8,40,72,104,488,456,136,168,200,232,424,392,360,328,264},{297,9,41..., dimensions={0} | all-to-all | bytes 262144 | tf_op jit(solution)/shard_map/all_to_all | solution.py:212
  32.1 0.0 collective-permute-done.other_ref
  32.1 0.6 shard_map.62
  32.7 9.2 %all_to_all.21.parts_ref = f32[8,4,128]{2,1,0:T(4,128)S(1)} all-to-all(f32[8,4,128]{2,1,0:T(4,128)S(1)} %shard_map.62), channel_id=1, replica_groups={{5,0,2,6,1,3,7,4},{13,8,10,14,9,11,15,12},{21,16,18,22,17,19,23,20},{29..., dimensions={0} | all-to-all | bytes 32768 | tf_op jit(solution)/shard_map/all_to_all | solution.py:245
  42.0 1.5 %shard_map.63 = (f32[4,128]{1,0:T(4,128)S(1)}, f32[4,128]{1,0:T(4,128)S(1)}, f32[16,128]{1,0:T(8,128)S(1)}, f32[2,16,128]{2,1,0:T(8,128)S(1)}, f32[512,2048]{1,0:T(8,128)S(1)}) custom-call(bf16[256,2048]{1,0:T(8,128)(2,1)S(1)} %get-tuple-element.19.values_ref, f32[256,2048]{1,0:T(8,128)S(1)} %collective-permute-done.other_ref, ...), custom_call_target="tpu_custom_call" | custom-call | tf_op jit(solution)/shard_map/pallas_call | solution.py:246
  43.5 3.2 %all-gather.2 = f32[32,128]{1,0:T(8,128)S(1)} all-gather(f32[16,128]{1,0:T(8,128)S(1)} %get-tuple-element.27), channel_id=4, replica_groups={{0,16},{8,24},{32,48},{40,56},{64,80},{72,88},{96,112},{104,120},{128,1..., dimensions={0}, use_global_device_ids=true | all-gather | bytes 24576 | tf_op jit(solution)/shard_map/all_gather | solution.py:211
  46.8 15.8 %all_to_all.22.z_ref = f32[16,16,128]{2,1,0:T(8,128)S(1)} all-to-all(f32[16,16,128]{2,1,0:T(8,128)S(1)} %shard_map.64), channel_id=1, replica_groups={{296,8,40,72,104,488,456,136,168,200,232,424,392,360,328,264},{297,9,41..., dimensions={0} | all-to-all | bytes 262144 | tf_op jit(solution)/shard_map/all_to_all | solution.py:212
  62.5 0.4 shard_map.65
  63.0 8.6 %all_to_all.23.parts_ref = f32[8,4,128]{2,1,0:T(4,128)S(1)} all-to-all(f32[8,4,128]{2,1,0:T(4,128)S(1)} %get-tuple-element.30), channel_id=1, replica_groups={{5,0,2,6,1,3,7,4},{13,8,10,14,9,11,15,12},{21,16,18,22,17,19,23,20},{29..., dimensions={0} | all-to-all | bytes 32768 | tf_op jit(solution)/shard_map/all_to_all | solution.py:267
  71.6 1.8 %all-gather.3 = f32[48,128]{1,0:T(8,128)S(1)} all-gather(f32[24,128]{1,0:T(8,128)S(1)} %shard_map.66), channel_id=5, replica_groups={{8,0},{24,16},{40,32},{56,48},{72,64},{88,80},{104,96},{120,112},{136,1..., dimensions={0}, use_global_device_ids=true | all-gather | bytes 36864 | tf_op jit(solution)/shard_map/all_gather | solution.py:281
  73.4 0.6 shard_map.67
  (4 shorter events, 0.1 us)
Async XLA Ops:
  11.0 21.2 %collective-permute-start = (f32[256,2048]{1,0:T(8,128)S(1)}, f32[256,2048]{1,0:T(8,128)S(1)}, u32[]{:S(2)}, u32[]{:S(2)}) collective-permute-start(f32[256,2048]{1,0:T(8,128)S(1)} %get-tuple-element.22), channel_id=1, source_target_pairs={{0,8},{16,24},{32,40},{48,56},{64,72},{80,88},{96,104},{112,120},{... | collective-permute-start | bytes 6291464 | tf_op jit(solution)/shard_map/ppermute | solution.py:236

commit v8 on v6

--- a/solution.py
+++ b/solution.py
@@ -161,12 +161,11 @@
     lse = total_lse(z_ref, reserve_ref)
     spread_rows(scale_ref, pair_ref[0, pl.ds(strips, halves), :])
     put_parts(parts_ref, 0, weighted_sums(weighted_ref, pl.ds(0, rows), jnp.exp2(top_ref[...] - lse)))
-    for h in range(halves):
-        acc = jnp.zeros((LANES, LANES), jnp.float32)
-        for s in range(strips):
-            y = other_ref[strip(h), strip(s)] * scale_ref[strip(h), :]
-            acc = acc + y * jnp.exp2(y - lse[s : s + 1, :])
-        put_parts(parts_ref, halves + h, acc)
+    acc = jnp.zeros((rows, LANES), jnp.float32)
+    for s in range(strips):
+        y = other_ref[:, strip(s)] * scale_ref[...]
+        acc = acc + y * jnp.exp2(y - lse[s : s + 1, :])
+    put_parts(parts_ref, halves, acc)
 
 
 def last_spend_kernel(z_ref, reserve_ref, top_ref, weighted_ref, parts_ref, prices_ref):

time: 74.3 us -> 74.3 us (level)
  no operation moved by 1% of the time
where the time goes in v8:
time: 74.3 us; the launch traced here: 74 us
  blocking collectives  66.8 us (90%)
  Pallas kernels  5.22 us (7%)
  starting transfers between devices  1.28 us (2%)
    all_to_all x2, blocking collectives, along_z(): lax.all_to_all(own, ('adv', 'imp'), 0, 0, axis_index_groups=groups['z'],...  32.4 us
    all_to_all x2, blocking collectives, on_device(): lax.all_to_all(parts, 'imp', 0, 0, axis_index_groups=groups['imp'], tiled...  17.8 us
    all_gather x1, blocking collectives, on_device(): pair = lax.all_gather(send, 'adv', axis_index_groups=groups['cores'])  8.32 us
    all_gather x2, blocking collectives, along_z(): lax.all_gather(own, 'adv', axis_index_groups=groups['chips'])  6.42 us
    pallas_call x1, Pallas kernels, on_device(): pl.pallas_call(first_kernel, compiler_params=PARAMS, out_shape=(f32(strip...  2 us
    all_gather x1, blocking collectives, on_device(): lax.all_gather(done, 'adv', axis_index_groups=groups['cores'])  1.82 us
    pallas_call x1, Pallas kernels, on_device(): pl.pallas_call(next_kernel, compiler_params=PARAMS, out_shape=(f32(both,...  1.54 us
  transfers between devices with their start and end apart: 1, of which 0 were waited for; matrix products, arithmetic and copies ran while one was open for 0% of the time, Pallas kernels for 0%

profile of v8, /device:TPU:1, one launch (start us, length us, event | category | flops | bytes accessed | tf_op | source)
XLA Modules:
  0.0 74.0 jit_solution(16114187333459237209)
XLA Ops:
  0.6 2.0 %shard_map.59 = (f32[24,128]{1,0:T(8,128)S(1)}, f32[16,128]{1,0:T(8,128)S(1)}, f32[256,2048]{1,0:T(8,128)S(1)}, bf16[256,2048]{1,0:T(8,128)(2,1)S(1)}, f32[256,2048]{1,0:T(8,128)S(1)}, /*index=5*/f32[16,128]{1,0:T(8,128)S(1)}) custom-call(bf16[256,2048]{1,0:T(8,128)(2,1)} %values_hbm.1, f32[2,128]{1,0:T(2,128)} %bitcast.16, f32[2,128]{1,0:T(2,128)} %bitcast.17, ...), custom_call_target="tpu_custom_call" | custom-call | tf_op jit(solution)/shard_map/pallas_call | solution.py:213
  2.6 8.3 %all-gather = f32[48,128]{1,0:T(8,128)S(1)} all-gather(f32[24,128]{1,0:T(8,128)S(1)} %get-tuple-element.21.send_ref), channel_id=2, replica_groups={{0,8},{16,24},{32,40},{48,56},{64,72},{80,88},{96,104},{112,120},{128,1..., dimensions={0}, use_global_device_ids=true | all-gather | bytes 36864 | tf_op jit(solution)/shard_map/all_gather | solution.py:233
  11.0 1.3 %collective-permute-start = (f32[256,2048]{1,0:T(8,128)S(1)}, f32[256,2048]{1,0:T(8,128)S(1)}, u32[]{:S(2)}, u32[]{:S(2)}) collective-permute-start(f32[256,2048]{1,0:T(8,128)S(1)} %get-tuple-element.22), channel_id=1, source_target_pairs={{0,8},{16,24},{32,40},{48,56},{64,72},{80,88},{96,104},{112,120},{... | collective-permute-start | bytes 6291464 | tf_op jit(solution)/shard_map/ppermute | solution.py:235
  12.3 3.2 %all-gather.1 = f32[32,128]{1,0:T(8,128)S(1)} all-gather(f32[16,128]{1,0:T(8,128)S(1)} %shard_map.60), channel_id=3, replica_groups={{0,16},{8,24},{32,48},{40,56},{64,80},{72,88},{96,112},{104,120},{128,1..., dimensions={0}, use_global_device_ids=true | all-gather | bytes 24576 | tf_op jit(solution)/shard_map/all_gather | solution.py:210
  15.5 16.6 %all_to_all.20.z_ref = f32[16,16,128]{2,1,0:T(8,128)S(1)} all-to-all(f32[16,16,128]{2,1,0:T(8,128)S(1)} %shard_map.61), channel_id=1, replica_groups={{296,8,40,72,104,488,456,136,168,200,232,424,392,360,328,264},{297,9,41..., dimensions={0} | all-to-all | bytes 262144 | tf_op jit(solution)/shard_map/all_to_all | solution.py:211
  32.1 0.0 collective-permute-done.other_ref
  32.1 0.6 shard_map.62
  32.7 9.2 %all_to_all.21.parts_ref = f32[8,4,128]{2,1,0:T(4,128)S(1)} all-to-all(f32[8,4,128]{2,1,0:T(4,128)S(1)} %shard_map.62), channel_id=1, replica_groups={{5,0,2,6,1,3,7,4},{13,8,10,14,9,11,15,12},{21,16,18,22,17,19,23,20},{29..., dimensions={0} | all-to-all | bytes 32768 | tf_op jit(solution)/shard_map/all_to_all | solution.py:244
  42.0 1.5 %shard_map.63 = (f32[4,128]{1,0:T(4,128)S(1)}, f32[4,128]{1,0:T(4,128)S(1)}, f32[16,128]{1,0:T(8,128)S(1)}, f32[2,16,128]{2,1,0:T(8,128)S(1)}, f32[512,2048]{1,0:T(8,128)S(1)}) custom-call(bf16[256,2048]{1,0:T(8,128)(2,1)S(1)} %get-tuple-element.19.values_ref, f32[256,2048]{1,0:T(8,128)S(1)} %collective-permute-done.other_ref, ...), custom_call_target="tpu_custom_call" | custom-call | tf_op jit(solution)/shard_map/pallas_call | solution.py:245
  43.5 3.2 %all-gather.2 = f32[32,128]{1,0:T(8,128)S(1)} all-gather(f32[16,128]{1,0:T(8,128)S(1)} %get-tuple-element.27), channel_id=4, replica_groups={{0,16},{8,24},{32,48},{40,56},{64,80},{72,88},{96,112},{104,120},{128,1..., dimensions={0}, use_global_device_ids=true | all-gather | bytes 24576 | tf_op jit(solution)/shard_map/all_gather | solution.py:210
  46.8 15.8 %all_to_all.22.z_ref = f32[16,16,128]{2,1,0:T(8,128)S(1)} all-to-all(f32[16,16,128]{2,1,0:T(8,128)S(1)} %shard_map.64), channel_id=1, replica_groups={{296,8,40,72,104,488,456,136,168,200,232,424,392,360,328,264},{297,9,41..., dimensions={0} | all-to-all | bytes 262144 | tf_op jit(solution)/shard_map/all_to_all | solution.py:211
  62.5 0.4 shard_map.65
  63.0 8.6 %all_to_all.23.parts_ref = f32[8,4,128]{2,1,0:T(4,128)S(1)} all-to-all(f32[8,4,128]{2,1,0:T(4,128)S(1)} %get-tuple-element.30), channel_id=1, replica_groups={{5,0,2,6,1,3,7,4},{13,8,10,14,9,11,15,12},{21,16,18,22,17,19,23,20},{29..., dimensions={0} | all-to-all | bytes 32768 | tf_op jit(solution)/shard_map/all_to_all | solution.py:266
  71.6 1.8 %all-gather.3 = f32[48,128]{1,0:T(8,128)S(1)} all-gather(f32[24,128]{1,0:T(8,128)S(1)} %shard_map.66), channel_id=5, replica_groups={{0,8},{16,24},{32,40},{48,56},{64,72},{80,88},{96,104},{112,120},{128,1..., dimensions={0}, use_global_device_ids=true | all-gather | bytes 36864 | tf_op jit(solution)/shard_map/all_gather | solution.py:280
  73.4 0.6 shard_map.67
  (4 shorter events, 0.1 us)
Async XLA Ops:
  11.0 21.2 %collective-permute-start = (f32[256,2048]{1,0:T(8,128)S(1)}, f32[256,2048]{1,0:T(8,128)S(1)}, u32[]{:S(2)}, u32[]{:S(2)}) collective-permute-start(f32[256,2048]{1,0:T(8,128)S(1)} %get-tuple-element.22), channel_id=1, source_target_pairs={{0,8},{16,24},{32,40},{48,56},{64,72},{80,88},{96,104},{112,120},{... | collective-permute-start | bytes 6291464 | tf_op jit(solution)/shard_map/ppermute | solution.py:235
